TPU v7x, 32 devices: a whole 2x2x4 slice. The times are simulated.
32 devices in a mesh: head: 2 (over x), blk: 16 (over z, y, core).
Axes of the slice: x: 2, y: 2, z: 4, core: 2. Of those that a mesh axis runs over, the one named last changes fastest.
Arguments:
- tokens: bfloat16 [2, 2048, 1024], P(None, ('head', 'blk')), may hold values from -6 to 6
- cotangent: bfloat16 [2, 2048, 1024], P(None, ('head', 'blk')), may hold values from -6 to 6
- ln1_gain: bfloat16 [1024], P(('head', 'blk')), may hold values from 0.5 to 1.5
- ln1_bias: bfloat16 [1024], P(('head', 'blk')), may hold values from -3 to 3
- w_query: bfloat16 [1024, 1024], P(('head', 'blk')), may hold values from -0.3125 to 0.3125
- w_key: bfloat16 [1024, 1024], P(('head', 'blk')), may hold values from -0.3125 to 0.3125
- w_value: bfloat16 [1024, 1024], P(('head', 'blk')), may hold values from -0.1875 to 0.1875
- w_out: bfloat16 [1024, 1024], P(('head', 'blk')), may hold values from -0.5 to 0.5
- ln2_gain: bfloat16 [1024], P(('head', 'blk')), may hold values from 0.5 to 1.5
- ln2_bias: bfloat16 [1024], P(('head', 'blk')), may hold values from -3 to 3
- w_inner: bfloat16 [1024, 4096], P(('head', 'blk')), may hold values from -0.1875 to 0.1875
- w_outer: bfloat16 [4096, 1024], P(('head', 'blk')), may hold values from -0.125 to 0.125
Outputs:
- result: bfloat16 [2, 2048, 1024], P(None, ('head', 'blk'))
- grad_tokens: float32 [2, 2048, 1024], P(None, ('head', 'blk'))
- grad_ln1_gain: float32 [1024], P(('head', 'blk'))
- grad_ln1_bias: float32 [1024], P(('head', 'blk'))
- grad_w_query: float32 [1024, 1024], P(('head', 'blk'))
- grad_w_key: float32 [1024, 1024], P(('head', 'blk'))
- grad_w_value: float32 [1024, 1024], P(('head', 'blk'))
- grad_w_out: float32 [1024, 1024], P(('head', 'blk'))
- grad_ln2_gain: float32 [1024], P(('head', 'blk'))
- grad_ln2_bias: float32 [1024], P(('head', 'blk'))
- grad_w_inner: float32 [1024, 4096], P(('head', 'blk'))
- grad_w_outer: float32 [4096, 1024], P(('head', 'blk'))
All inputs are finite; a program needn't handle non-finite values.
Results may differ from a plain program's by a relative error of at most 0.015.
The roundings to bfloat16 on the way count: a program that leaves them out, or rounds other values in their place, can miss the bound.
Values may be sent and summed in bfloat16 or wider, within the bound.
No kernel may reach another device: no remote copies, remote signals or barrier semaphores. Data moves between devices by JAX's collectives and lax.ppermute only.
A program may use at most 320 MiB of HBM per device.

v0:
```python
import functools
import math

import jax
import jax.numpy as jnp
from jax import lax
from jax.experimental import pallas as pl
from jax.experimental.pallas import tpu as pltpu
from jax.sharding import Mesh
from jax.sharding import PartitionSpec as P

HD = 128
TILE = 256
SCALE = HD ** (-0.5)
MASKED = -1e30
eps_norm = 1e-05
gelu_coef = math.sqrt(2.0 / math.pi)
BF = jnp.bfloat16
F32 = jnp.float32
AXES = ("x", "za", "zb", "zl", "y", "c")
T_AXES = ("x", "za", "zb")
W_AXES = ("zl", "y", "c")


def mm(a, b):
    return jnp.dot(a, b, preferred_element_type=F32)


def mm_nt(a, b):
    return lax.dot_general(a, b, (((1,), (1,)), ((), ())), preferred_element_type=F32)


def mm_tn(a, b):
    return lax.dot_general(a, b, (((0,), (0,)), ((), ())), preferred_element_type=F32)


def norm_stats(values):
    centered = values - jnp.mean(values, -1, keepdims=True)
    inverse = lax.rsqrt(jnp.mean(centered * centered, -1, keepdims=True) + eps_norm)
    return centered * inverse, inverse


def norm_back(grad_normed, scaled, inverse, gain):
    g = grad_normed * gain
    return inverse * (
        g - jnp.mean(g, -1, keepdims=True) - scaled * jnp.mean(g * scaled, -1, keepdims=True)
    )


def swap(v, axis):
    return lax.ppermute(v, axis, [(0, 1), (1, 0)])


def pick(v, index, axis=0):
    return lax.dynamic_index_in_dim(v, index, axis, keepdims=False)


def pair_gather(v, axis):
    other = swap(v, axis)
    first = lax.axis_index(axis) == 0
    return jnp.stack([jnp.where(first, v, other), jnp.where(first, other, v)])


def pair_scatter(v, axis, dim):
    me = lax.axis_index(axis)
    return pick(v, me, dim) + swap(pick(v, 1 - me, dim).astype(BF), axis).astype(F32)


def after(v, *others):
    return lax.optimization_barrier((v,) + others)[0]


def t_gather(v):
    if lax.axis_size("za") * lax.axis_size("zb") != 2:
        return lax.all_gather(v, T_AXES, axis=0, tiled=False)
    x, z = lax.axis_index("x"), lax.axis_index("za")
    over_x, over_z = swap(v, "x"), swap(v, "za")
    out = jnp.zeros((4,) + v.shape, v.dtype)
    for part, at in (
        (v, 2 * x + z),
        (over_x, 2 * (1 - x) + z),
        (over_z, 2 * x + 1 - z),
        (swap(over_z, "x"), 2 * (1 - x) + 1 - z),
    ):
        out = lax.dynamic_update_index_in_dim(out, part, at, 0)
    return out


def t_scatter(v):
    if lax.axis_size("za") * lax.axis_size("zb") != 2:
        return lax.psum_scatter(v, T_AXES, scatter_dimension=0, tiled=False)
    v = pair_scatter(v.reshape((2, 2) + v.shape[1:]), "x", 0)
    return pair_scatter(v, "za", 0)


def plane_gather(v):
    half = v.shape[0] // 2
    a, b = v[:half], v[half:]
    a = jnp.stack([a, swap(a, "zl")])
    b = jnp.stack([b, swap(b, "y")])
    a = jnp.stack([a, swap(a, "y")])
    b = jnp.stack([b, swap(b, "zl")])
    both = jnp.stack([a, b])
    return jnp.stack([both, swap(both, "c")]).reshape(8 * v.shape[0], v.shape[1])


def plane_scatter(v):
    rows, width = v.shape
    v = v.reshape(2, 2, 2, 2, rows // 16, width)

    def fold(u, axis):
        return u[0] + swap(u[1].astype(BF), axis).astype(F32)

    v = fold(v, "c")
    a, b = v[0], v[1]
    a = fold(a, "y")
    b = fold(b, "zl")
    a = fold(a, "zl")
    b = fold(b, "y")
    return jnp.concatenate([a, b], 0)


def shares(count, body):
    if count <= 2:
        for k in range(count):
            body(k)
    else:
        lax.fori_loop(0, count, lambda k, c: (body(k), c)[1], 0)


def mask_of(count, q_tile, k_tile, q_share, k_share):
    rows = lax.broadcasted_iota(jnp.int32, (TILE, TILE), 0) + q_tile * TILE
    cols = lax.broadcasted_iota(jnp.int32, (TILE, TILE), 1) + k_tile * TILE
    q_pos = (lax.shift_right_logical(rows, 6) * count + q_share) * 64 + (rows & 63)
    k_pos = (lax.shift_right_logical(cols, 6) * count + k_share) * 64 + (cols & 63)
    return k_pos <= q_pos


def forward_kernel(count, meta, q_ref, k_ref, v_ref, o_ref, of_ref, lse_ref, qa, ka, va, s_ref):
    blocks = q_ref.shape[0]
    for j in range(blocks):
        slot = meta[j]
        rows = pl.ds(j * 64, 64)
        qa[rows, :] = q_ref[slot]

        def place(k, rows=rows, slot=slot):
            ka[k, rows, :] = k_ref[k, slot]
            va[k, rows, :] = v_ref[k, slot]

        shares(count, place)
    mine = meta[blocks]
    tiles = blocks * 64 // TILE
    for t in range(tiles):
        q = qa[pl.ds(t * TILE, TILE), :]
        top = jnp.full((TILE, 1), MASKED, F32)
        for u in range(t + 1):
            cols = pl.ds(u * TILE, TILE)

            def score(k, top, u=u, cols=cols):
                s = mm_nt(q, ka[k, cols, :]) * SCALE
                if u == t:
                    s = jnp.where(mask_of(count, t, u, mine, meta[blocks + 1 + k]), s, MASKED)
                s_ref[k * tiles + u] = s
                return jnp.maximum(top, jnp.max(s, -1, keepdims=True))

            if count <= 2:
                for k in range(count):
                    top = score(k, top)
            else:
                top = lax.fori_loop(0, count, score, top)
        total = jnp.zeros((TILE, 1), F32)
        for u in range(t + 1):

            def expo(k, total, u=u):
                p = jnp.exp(s_ref[k * tiles + u] - top)
                s_ref[k * tiles + u] = p
                return total + jnp.sum(p, -1, keepdims=True)

            if count <= 2:
                for k in range(count):
                    total = expo(k, total)
            else:
                total = lax.fori_loop(0, count, expo, total)
        inverse = 1.0 / total
        out = jnp.zeros((TILE, HD), F32)
        for u in range(t + 1):
            cols = pl.ds(u * TILE, TILE)

            def weigh(k, out, u=u, cols=cols):
                p = (s_ref[k * tiles + u] * inverse).astype(BF)
                return out + mm(p, va[k, cols, :])

            if count <= 2:
                for k in range(count):
                    out = weigh(k, out)
            else:
                out = lax.fori_loop(0, count, weigh, out)
        rows = pl.ds(t * TILE, TILE)
        of_ref[rows, :] = out
        o_ref[rows, :] = out.astype(BF)
        lse_ref[rows, :] = jnp.broadcast_to(top + jnp.log(total), (TILE, HD))


def attention_forward(count, meta, q, k, v):
    blocks = q.shape[0]
    rows = blocks * 64
    tiles = rows // TILE
    vm = pl.BlockSpec(memory_space=pltpu.VMEM)
    pairs = tiles * (tiles + 1) // 2 * count
    return pl.pallas_call(
        functools.partial(forward_kernel, count),
        in_specs=[pl.BlockSpec(memory_space=pltpu.SMEM), vm, vm, vm],
        out_specs=[vm] * 6,
        out_shape=[
            jax.ShapeDtypeStruct((rows, HD), BF),
            jax.ShapeDtypeStruct((rows, HD), F32),
            jax.ShapeDtypeStruct((rows, HD), F32),
            jax.ShapeDtypeStruct((rows, HD), BF),
            jax.ShapeDtypeStruct((count, rows, HD), BF),
            jax.ShapeDtypeStruct((count, rows, HD), BF),
        ],
        scratch_shapes=[pltpu.VMEM((count * tiles, TILE, TILE), F32)],
        cost_estimate=pl.CostEstimate(
            flops=pairs * TILE * TILE * HD * 4,
            bytes_accessed=rows * HD * 2 * (2 + 4 * count) + rows * HD * 8,
            transcendentals=pairs * TILE * TILE,
        ),
        compiler_params=pltpu.CompilerParams(vmem_limit_bytes=(16 if count <= 2 else 52) << 20),
        name="attention_forward",
    )(meta, q, k, v)


def backward_kernel(count, meta, q_ref, k_ref, v_ref, go_ref, of_ref, lse_ref, gq_ref, gk, gv):
    rows_all = q_ref.shape[0]
    blocks = rows_all // 64
    mine = meta[blocks]
    tiles = rows_all // TILE

    def zero(k):
        gk[k] = jnp.zeros((rows_all, HD), F32)
        gv[k] = jnp.zeros((rows_all, HD), F32)

    shares(count, zero)
    for t in range(tiles):
        rows = pl.ds(t * TILE, TILE)
        q = q_ref[rows, :]
        go = go_ref[rows, :]
        delta = jnp.sum(go.astype(F32) * of_ref[rows, :], -1, keepdims=True)
        lse = lse_ref[rows, :][:, :1]
        gq = jnp.zeros((TILE, HD), F32)
        for u in range(t + 1):
            cols = pl.ds(u * TILE, TILE)

            def one(k, gq, u=u, cols=cols):
                kk = k_ref[k, cols, :]
                p = jnp.exp(mm_nt(q, kk) * SCALE - lse)
                if u == t:
                    p = jnp.where(mask_of(count, t, u, mine, meta[blocks + 1 + k]), p, 0.0)
                gv[k, cols, :] += mm_tn(p.astype(BF), go)
                ds = (p * (mm_nt(go, v_ref[k, cols, :]) - delta)).astype(BF)
                gk[k, cols, :] += mm_tn(ds, q)
                return gq + mm(ds, kk)

            if count <= 2:
                for k in range(count):
                    gq = one(k, gq)
            else:
                gq = lax.fori_loop(0, count, one, gq)
        gq_ref[rows, :] = (gq * SCALE).astype(BF)

    def scale(k):
        gk[k] = gk[k] * SCALE

    shares(count, scale)


def attention_backward(count, meta, q, k, v, go, of, lse):
    rows = q.shape[0]
    tiles = rows // TILE
    vm = pl.BlockSpec(memory_space=pltpu.VMEM)
    pairs = tiles * (tiles + 1) // 2 * count
    return pl.pallas_call(
        functools.partial(backward_kernel, count),
        in_specs=[pl.BlockSpec(memory_space=pltpu.SMEM)] + [vm] * 6,
        out_specs=[vm] * 3,
        out_shape=[
            jax.ShapeDtypeStruct((rows, HD), BF),
            jax.ShapeDtypeStruct((count, rows, HD), F32),
            jax.ShapeDtypeStruct((count, rows, HD), F32),
        ],
        cost_estimate=pl.CostEstimate(
            flops=pairs * TILE * TILE * HD * 10,
            bytes_accessed=rows * HD * (16 + 12 * count),
            transcendentals=pairs * TILE * TILE,
        ),
        compiler_params=pltpu.CompilerParams(vmem_limit_bytes=(16 if count <= 2 else 52) << 20),
        name="attention_backward",
    )(meta, q, k, v, go, of, lse)


def reorder_kernel(meta, g_ref, out_ref):
    for j in range(g_ref.shape[0]):
        out_ref[meta[j]] = g_ref[j]


def reorder(meta, g):
    vm = pl.BlockSpec(memory_space=pltpu.VMEM)
    return pl.pallas_call(
        reorder_kernel,
        in_specs=[pl.BlockSpec(memory_space=pltpu.SMEM), vm],
        out_specs=vm,
        out_shape=jax.ShapeDtypeStruct(g.shape, g.dtype),
        cost_estimate=pl.CostEstimate(flops=0, bytes_accessed=4 * g.size, transcendentals=0),
        compiler_params=pltpu.CompilerParams(vmem_limit_bytes=8 << 20),
        name="reorder",
    )(meta, g)


def on_device(
    roles,
    tokens,
    cotangent,
    ln1_gain,
    ln1_bias,
    w_query,
    w_key,
    w_value,
    w_out,
    ln2_gain,
    ln2_bias,
    w_inner,
    w_outer,
):
    small, seq_axis, hd_axes, sh_axes, own_axes = roles
    planes = math.prod(lax.axis_size(a) for a in T_AXES)
    count = math.prod(lax.axis_size(a) for a in sh_axes)
    devices = 8 * planes
    seqs, tok, width = tokens.shape
    rows = seqs * tok
    per = w_query.shape[0]
    unit = w_outer.shape[0]
    seq = lax.axis_index(seq_axis)
    share = lax.axis_index(sh_axes)

    block = jnp.stack([pick(tokens, seq), swap(pick(tokens, 1 - seq), seq_axis)])
    if small:
        on_x, on_z, on_y = (swap(block, a) for a in hd_axes)
        on_xz, on_xy, on_zy = swap(on_x, "zl"), swap(on_y, "x"), swap(on_z, "y")
        on_xyz = swap(on_xz, "y")
        seen = jnp.stack([block, on_y, on_z, on_zy, on_x, on_xy, on_xz, on_xyz])
    else:
        seen = lax.all_gather(block, hd_axes, axis=0, tiled=False)
    at = jnp.arange(16, dtype=jnp.int32)
    if small:
        at_x, at_za, at_zl, at_y = at // 8, at // 4 % 2, at // 2 % 2, at % 2
        x, zl, y = (lax.axis_index(a) for a in hd_axes)
        slots = ((at_x ^ x) * 4 + (at_zl ^ zl) * 2 + (at_y ^ y)) * 2 + (at_za ^ seq)
    else:
        slots = at % 8 * 2 + (at // 8 ^ seq)

    gains = jnp.concatenate([ln1_gain, ln1_bias, ln2_gain, ln2_bias])
    gains = jnp.broadcast_to(jnp.pad(gains, (0, HD - gains.shape[0])), (8, 1, HD))
    head_w = jnp.stack([w_query, w_key, w_value]).reshape(3, per, 8, HD).transpose(2, 0, 1, 3)
    head_w = jnp.concatenate([head_w.reshape(8, 3 * per, HD), gains], 1)
    head_w = lax.all_to_all(head_w, hd_axes, 0, 0, tiled=True)
    head_w = pair_gather(head_w, seq_axis)
    for axis in reversed(sh_axes):
        if lax.axis_size(axis) == 2:
            head_w = pair_gather(head_w, axis)
        else:
            head_w = lax.all_gather(head_w, axis, axis=0, tiled=False)
    if small:
        head_w = head_w.reshape(2, 2, 2, 4, 3 * per + 1, HD).transpose(2, 1, 3, 0, 4, 5)
    else:
        head_w = head_w.reshape(count, 16, 3 * per + 1, HD).transpose(1, 0, 2, 3)
    head_w = head_w.reshape(devices, 3 * per + 1, HD)
    gains = head_w[:, -1, : 4 * per].reshape(devices, 4, per).transpose(1, 0, 2)
    gains = gains.reshape(4, width).astype(F32)
    gain_one, bias_one, gain_two, bias_two = gains[0], gains[1], gains[2], gains[3]
    head_w = head_w[:, :-1].reshape(devices, 3, per, HD).transpose(0, 2, 1, 3)
    head_w = head_w.reshape(width, 3 * HD)

    inner_w = w_inner.reshape(per, planes, 8, unit).transpose(2, 0, 1, 3)
    inner_w = lax.all_to_all(inner_w.reshape(8, per, planes * unit), W_AXES, 0, 0, tiled=True)
    inner_w = t_gather(after(inner_w, seen)).reshape(width, planes * unit)
    outer_w = t_gather(w_outer).reshape(planes * unit, width)
    grad_plane = plane_gather(after(cotangent, seen).reshape(rows, width))

    out_w = lax.all_gather(w_out, AXES, axis=0, tiled=True)
    qkv_w = jnp.concatenate([w_query, w_key, w_value], 1)
    qkv_w = lax.all_gather(after(qkv_w, seen), AXES, axis=0, tiled=True)

    normed, _ = norm_stats(seen.reshape(-1, width).astype(F32))
    h1 = (normed * gain_one + bias_one).astype(BF)
    qkv = mm(h1, head_w).astype(BF)
    query = qkv[:, :HD].reshape(16, tok, HD)
    kv = qkv[:, HD:]
    if count == 2:
        kv = jnp.stack([kv, swap(kv, "c")])
        order = jnp.stack([share, 1 - share])
    else:
        kv = lax.all_gather(kv, sh_axes, axis=0, tiled=False)
        order = jnp.arange(count)
    kv = kv.reshape(count, 16, tok, 2 * HD)
    meta = jnp.concatenate([slots, share.reshape(1), order]).astype(jnp.int32)
    out, out_f, lse, q_at, k_at, v_at = attention_forward(
        count, meta, query, kv[..., :HD], kv[..., HD:]
    )

    def to_tokens(v):
        v = lax.all_to_all(v, own_axes, 0, 0, tiled=True)
        n = v.shape[-1] // HD
        if small:
            v = v.reshape(2, 2, 4, tok, n, HD).transpose(1, 3, 4, 0, 2, 5)
        else:
            v = v.reshape(2, 8, tok, n, HD).transpose(0, 2, 3, 1, 4)
        return v.reshape(2, tok, n, 8 * HD)

    mixed = to_tokens(out.reshape(16, tok, HD)).reshape(rows, width)
    flat_in = tokens.reshape(rows, width).astype(F32)
    middle = flat_in + mm(mixed, out_w)
    scaled_two, inverse_two = norm_stats(middle)
    h2 = plane_gather((scaled_two * gain_two + bias_two).astype(BF))

    inner = mm(h2, inner_w)
    bent = jnp.tanh(gelu_coef * (inner + 0.044715 * inner * inner * inner))
    hidden = (0.5 * inner * (1.0 + bent)).astype(BF)
    slope = 0.5 * (1.0 + bent) + 0.5 * inner * (1.0 - bent * bent) * gelu_coef * (
        1.0 + 3.0 * 0.044715 * inner * inner
    )
    grad_inner = (mm_nt(grad_plane, outer_w) * slope).astype(BF)
    grad_h2 = plane_scatter(mm_nt(grad_inner, inner_w))
    grad_outer = mm_tn(hidden, grad_plane).reshape(planes, unit, width)
    grad_outer = t_scatter(grad_outer)
    grad_in = mm_tn(h2, grad_inner).reshape(planes, 8 * per, planes * unit)
    grad_in = t_scatter(grad_in).astype(BF).reshape(8, per, planes * unit)
    result = plane_scatter(mm(hidden, outer_w))

    grad_out = cotangent.reshape(rows, width).astype(F32)
    grad_middle = grad_out + norm_back(grad_h2, scaled_two, inverse_two, gain_two)
    branch = grad_middle.astype(BF)
    go = mm_nt(branch, out_w).astype(BF)
    if small:
        go = go.reshape(2, tok, 2, 4, HD).transpose(2, 0, 3, 1, 4)
    else:
        go = go.reshape(2, tok, 8, HD).transpose(0, 2, 1, 3)
    go = lax.all_to_all(go.reshape(16, tok, HD), own_axes, 0, 0, tiled=True)
    go = go.reshape(16 * tok, HD)

    gq, gk, gv = attention_backward(count, meta, q_at, k_at, v_at, go, out_f, lse)
    gkv = jnp.concatenate([gk, gv], -1)
    if count == 2:
        gkv = gkv[0] + swap(gkv[1].astype(BF), "c").astype(F32)
    else:
        gkv = lax.psum_scatter(gkv, sh_axes, scatter_dimension=0, tiled=False)
    grads = jnp.concatenate([gq, gkv.astype(BF)], -1).reshape(16, tok, 3 * HD)
    grads, result, grad_in, grad_outer = lax.optimization_barrier(
        (grads, result, grad_in, grad_outer)
    )
    back = to_tokens(grads).reshape(rows, 3 * width)
    result = (middle + result).astype(BF)
    grad_in = lax.all_to_all(after(grad_in, back), W_AXES, 0, 0, tiled=True)
    grad_in = grad_in.reshape(8, per, planes, unit).transpose(1, 2, 0, 3)
    grad_in = grad_in.reshape(per, devices * unit).astype(F32)

    head_g = mm_tn(h1, reorder(meta, grads).reshape(16 * tok, 3 * HD))
    head_g = head_g.reshape(tuple(lax.axis_size(a) for a in AXES) + (per, 3 * HD))
    dims = list(AXES)
    for axis in sh_axes[::-1] + (seq_axis,):
        dim = dims.index(axis)
        dims.remove(axis)
        if lax.axis_size(axis) == 2:
            head_g = pair_scatter(head_g, axis, dim)
        else:
            head_g = lax.psum_scatter(head_g, axis, scatter_dimension=dim, tiled=False)
    head_g = head_g.astype(BF).reshape(8, per, 3 * HD)
    head_g = lax.all_to_all(head_g, hd_axes, 0, 0, tiled=True)
    head_g = head_g.reshape(8, per, 3, HD).transpose(2, 1, 0, 3).reshape(3, per, width)
    head_g = head_g.astype(F32)

    grad_out_w = mm_tn(mixed, branch).reshape(planes, 2, 2, 2, per, width)
    grad_out_w = pair_scatter(grad_out_w, "c", 3)
    grad_out_w = pair_scatter(grad_out_w, "y", 2)
    grad_out_w = pair_scatter(grad_out_w, "zl", 1)
    grad_out_w = t_scatter(grad_out_w)

    scaled_one, inverse_one = norm_stats(flat_in)
    grad_h1 = mm_nt(back, qkv_w)
    grad_input = grad_middle + norm_back(grad_h1, scaled_one, inverse_one, gain_one)

    sums = jnp.stack(
        [
            jnp.sum(grad_h1 * scaled_one, 0),
            jnp.sum(grad_h1, 0),
            jnp.sum(grad_h2 * scaled_two, 0),
            jnp.sum(grad_h2, 0),
        ]
    )
    sums = sums.reshape(4, devices, per).transpose(1, 0, 2).reshape(devices, 4 * per)
    sums = lax.all_to_all(sums, AXES, 0, 0, tiled=True)
    sums = jnp.sum(sums, 0).reshape(4, per)
    return (
        result.reshape(seqs, tok, width),
        grad_input.reshape(seqs, tok, width),
        sums[0],
        sums[1],
        head_g[0],
        head_g[1],
        head_g[2],
        grad_out_w,
        sums[2],
        sums[3],
        grad_in,
        grad_outer,
    )


class Arriving:
    def __init__(self, ref, copy):
        self.ref, self.copy = ref, copy
        self.shape, self.dtype = ref.shape, ref.dtype

    def __getitem__(self, index):
        if self.copy is not None:
            self.copy.wait()
            self.copy = None
        return self.ref[index]


class Leaving:
    def __init__(self, ref, target, move):
        self.ref, self.target, self.move, self.pushed = ref, target, move, False
        self.shape, self.dtype = ref.shape, ref.dtype

    def __getitem__(self, index):
        return self.ref[index]

    def __setitem__(self, index, value):
        self.ref[index] = value

    def push(self, rows=None):
        self.pushed = True
        if rows is None:
            self.move(self.ref, self.target)
        else:
            self.move(self.ref.at[rows], self.target.at[rows])


def call(kernel, outs, ins, coords=None, raw=(), save=(), scratch=(), eager=False, name=None):
    hbm = pl.BlockSpec(memory_space=pltpu.HBM)
    outs = [tuple(o) + ("far",) * (3 - len(o)) for o in outs]
    far = [i for i in range(len(ins)) if i not in raw]
    lead = 0 if coords is None else 1
    late = [i for i, o in enumerate(outs) if o[2] == "far"]
    extra = [pltpu.VMEM(ins[i].shape, ins[i].dtype) for i in far]
    extra += [pltpu.VMEM(outs[i][0], outs[i][1]) for i in late]
    extra.append(pltpu.SemaphoreType.DMA((len(far) + 4 * len(late) + len(save),)))
    count_in, count_out = len(ins), len(outs) + len(save)

    def body(*refs):
        front, refs = refs[:lead], refs[lead:]
        got, put = list(refs[:count_in]), list(refs[count_in : count_in + count_out])
        work = refs[count_in + count_out :]
        own, work = work[: len(scratch)], work[len(scratch) :]
        started = []

        def move(source, target):
            copy = pltpu.make_async_copy(source, target, work[-1].at[len(started)])
            copy.start()
            started.append(copy)
            return copy

        for n, i in enumerate(far):
            got[i] = Arriving(work[n], move(got[i], work[n]))
        leaving = []
        for n, i in enumerate(save):
            got[i].copy.wait()
            got[i].copy = None
            leaving.append(move(got[i].ref, put[len(outs) + n]))
        if eager:
            for i in far:
                got[i].copy.wait()
                got[i].copy = None
        inside = put[: len(outs)]
        for n, i in enumerate(late):
            inside[i] = Leaving(
                work[len(far) + n], put[i], lambda a, b: leaving.append(move(a, b))
            )
        kernel(*front, *got, *inside, *own)
        for i in late:
            if not inside[i].pushed:
                inside[i].push()
        for i in far:
            if got[i].copy is not None:
                got[i].copy.wait()
        for copy in leaving:
            copy.wait()

    specs = [hbm] * len(ins)
    if coords is not None:
        specs = [pl.BlockSpec(memory_space=pltpu.SMEM)] + specs
    saved = [jax.ShapeDtypeStruct(ins[i].shape, ins[i].dtype) for i in save]
    return pl.pallas_call(
        body,
        in_specs=specs,
        out_specs=[hbm] * count_out,
        out_shape=[jax.ShapeDtypeStruct(o[0], o[1]) for o in outs] + saved,
        scratch_shapes=list(scratch) + extra,
        cost_estimate=pl.CostEstimate(flops=0, bytes_accessed=0, transcendentals=0),
        compiler_params=pltpu.CompilerParams(vmem_limit_bytes=58 << 20),
        name=name,
    )(*([] if coords is None else [coords]), *ins)


def aligned(index, size):
    if isinstance(index, int):
        return pl.ds(index * size, size)
    return pl.ds(pl.multiple_of(index * size, size), size)


def pack_kernel(wq, wk, wv, g1, b1, g2, b2, w_inner, head, inner):
    per = wq.shape[0]
    gains = jnp.concatenate([g1[...], b1[...], g2[...], b2[...]], 1)
    for d in range(16):
        cols = pl.ds(((d >> 3) * 4 + (d & 3)) * HD, HD)
        for n, w in enumerate((wq, wk, wv)):
            head[d, pl.ds(n * per, per), :] = w[:, cols]
        head[d, pl.ds(3 * per, 16), :] = jnp.broadcast_to(gains, (16, HD))
    for w in range(8):
        for t in range(4):
            p = (w >> 2) * 16 + t * 4 + (w & 3)
            inner[w, :, pl.ds(t * HD, HD)] = w_inner[:, pl.ds(p * HD, HD)]


def norm_of(values):
    centered = values - jnp.mean(values, -1, keepdims=True)
    inverse = lax.rsqrt(jnp.mean(centered * centered, -1, keepdims=True) + eps_norm)
    return centered * inverse, inverse


def qkv_kernel(at, *refs):
    blocks, pieces = refs[:8], refs[8:10]
    h1, query, kv, gains, weights = refs[10:]
    x, za, zl, y, c = (at[i] for i in range(5))
    width = h1.shape[1]
    per = width // 32
    got = jnp.concatenate([p[d, 3 * per : 3 * per + 1, :] for p in pieces for d in range(16)], 0)
    line = lax.broadcasted_iota(jnp.int32, (32, width), 0)
    lane = lax.broadcasted_iota(jnp.int32, (32, width), 1)
    owner = (line & 15) * 2 + (c ^ (line >> 4))
    mine = lax.shift_right_logical(lane, 5) == owner
    source = lax.broadcasted_iota(jnp.int32, (HD, width), 0)
    target = lax.broadcasted_iota(jnp.int32, (HD, width), 1)
    for k in range(4):
        spread = jnp.where(source == k * per + (target & (per - 1)), 1.0, 0.0).astype(BF)
        gains[k : k + 1, :] = jnp.sum(jnp.where(mine, mm(got, spread), 0.0), 0, keepdims=True)
    gain, bias = gains[0:1, :], gains[1:2, :]
    for n, block in enumerate(blocks):
        xx, zz, yy = x ^ (n >> 2), zl ^ (n >> 1 & 1), y ^ (n & 1)
        for s in range(2):
            j = xx * 8 + (za ^ s) * 4 + zz * 2 + yy
            normed, _ = norm_of(block[s].astype(F32))
            h1[aligned(j, 64), :] = (normed * gain + bias).astype(BF)
    h1.push()
    for n, piece in enumerate(pieces):
        for d in range(16):
            for i in range(3):
                weights[aligned(2 * d + (c ^ n), per), pl.ds(i * HD, HD)] = piece[
                    d, pl.ds(i * per, per), :
                ]
    weights.push()
    for t in range(h1.shape[0] // TILE):
        rows = pl.ds(t * TILE, TILE)
        out = mm(h1[rows, :], weights[...]).astype(BF)
        query[rows, :] = out[:, :HD]
        kv[rows, :] = out[:, HD:]
        query.push(rows)
        kv.push(rows)


def causal(q_share, k_share):
    rows = lax.broadcasted_iota(jnp.int32, (TILE, TILE), 0)
    cols = lax.broadcasted_iota(jnp.int32, (TILE, TILE), 1)
    q_pos = (lax.shift_right_logical(rows, 6) * 2 + q_share) * 64 + (rows & 63)
    k_pos = (lax.shift_right_logical(cols, 6) * 2 + k_share) * 64 + (cols & 63)
    return k_pos <= q_pos


def fine_forward_kernel(at, query, own, other, out, out_f, lse, s_ref):
    tiles = query.shape[0] // TILE
    c = at[4]
    both = (own, other)

    def tile(t, carry):
        rows = aligned(t, TILE)
        q = query[rows, :]

        def score(u, top, masked):
            for n in range(2):
                s = mm_nt(q, both[n][aligned(u, TILE), pl.ds(0, HD)]) * SCALE
                if masked:
                    s = jnp.where(causal(c, c if n == 0 else 1 - c), s, MASKED)
                s_ref[u * 2 + n] = s
                top = jnp.maximum(top, jnp.max(s, -1, keepdims=True))
            return top

        top = jnp.full((TILE, 1), MASKED, F32)
        for u in range(t + 1):
            top = score(u, top, u == t)

        def expo(u, total):
            for n in range(2):
                p = jnp.exp(s_ref[u * 2 + n] - top)
                s_ref[u * 2 + n] = p
                total = total + jnp.sum(p, -1, keepdims=True)
            return total

        total = jnp.zeros((TILE, 1), F32)
        for u in range(t + 1):
            total = expo(u, total)
        inverse = 1.0 / total

        def weigh(u, acc):
            for n in range(2):
                p = (s_ref[u * 2 + n] * inverse).astype(BF)
                acc = acc + mm(p, both[n][aligned(u, TILE), pl.ds(HD, HD)])
            return acc

        acc = jnp.zeros((TILE, HD), F32)
        for u in range(t + 1):
            acc = weigh(u, acc)
        out_f[rows, :] = acc
        out[pl.ds(t * (TILE // 64), TILE // 64)] = acc.astype(BF).reshape(TILE // 64, 64, HD)
        lse[rows, :] = jnp.broadcast_to(top + jnp.log(total), (TILE, HD))
        out.push(pl.ds(t * (TILE // 64), TILE // 64))
        out_f.push(rows)
        lse.push(rows)
        return carry

    for t in range(tiles):
        tile(t, 0)


def place_w_out(at, pieces, out_w, sems):
    x, za, zl, y, c = (at[i] for i in range(5))
    copies = []
    for n, piece in enumerate(pieces):
        side = (zl ^ (n & 1)) * 4 + (y ^ (n >> 1 & 1)) * 2 + (c ^ (n >> 2))
        for i in range(4):
            p = (x ^ (i >> 1)) * 16 + (za ^ (i & 1)) * 8 + side
            copies.append(
                pltpu.make_async_copy(
                    piece.at[i], out_w.at[aligned(p, piece.shape[1]), :], sems.at[len(copies)]
                )
            )
            copies[-1].start()
    return copies


def middle_kernel(at, got, tokens, gains, *refs):
    pieces, (mixed, middle, scaled, inverse, h2, out_w, sems) = refs[:8], refs[8:]
    copies = place_w_out(at, pieces, out_w, sems)
    rows, width = middle.shape
    tok = rows // 2
    for s in range(16):
        head = (s >> 3) * 4 + (s & 3)
        mixed[pl.ds((s >> 2 & 1) * tok, tok), pl.ds(head * HD, HD)] = got[s]
    for s in range(2):
        middle[pl.ds(s * tok, tok), :] = tokens[s].astype(F32)
    for copy in copies:
        copy.wait()
    mixed.push()
    middle[...] += mm(mixed[...], out_w[...])
    middle.push()
    normed, inv = norm_of(middle[...])
    scaled[...] = normed
    inverse[...] = jnp.broadcast_to(inv, (rows, HD))
    h2[...] = (normed * gains[2:3, :] + gains[3:4, :]).astype(BF)


def inner_kernel(at, *refs):
    h2_parts, cot_parts, in_parts, out_parts = refs[:10], refs[10:20], refs[20:24], refs[24:28]
    h2_out, cot_out, outer_out, hidden, grad_inner, keep, send = refs[28:35]
    h2, cot, w_in, w_outer, sems = refs[35:]
    za, zl = at[1], at[2]
    copies = []

    def move(source, target):
        copy = pltpu.make_async_copy(source, target, sems.at[len(copies)])
        copy.start()
        copies.append(copy)

    for n in range(4):
        t = (za ^ (n >> 1)) * 2 + (zl ^ (n & 1))
        for i in range(2):
            rows = in_parts[n].shape[1]
            move(in_parts[n].at[i], w_in.at[aligned(i * 4 + t, rows), :])
    for n in range(4):
        t = (za ^ (n >> 1)) * 2 + (zl ^ (n & 1))
        move(out_parts[n], w_outer.at[aligned(t, out_parts[n].shape[0]), :])
    row = 0
    for part in cot_parts:
        move(part, cot.at[pl.ds(row, part.shape[0]), :])
        row += part.shape[0]
    row = 0
    for part in h2_parts:
        h2[pl.ds(row, part.shape[0]), :] = part[...]
        row += part.shape[0]
    for copy in copies[:8]:
        copy.wait()
    first = mm(h2[pl.ds(0, TILE), :], w_in[...])
    for copy in copies[8:22]:
        copy.wait()
    arrived = 22
    move(h2, h2_out)
    move(cot, cot_out)
    move(w_outer, outer_out)
    half = h2.shape[0] // 2

    def tile(t, carry):
        rows = aligned(t, TILE)
        u = first if t == 0 else mm(h2[rows, :], w_in[...])
        squared = u * u
        bent = jnp.tanh(gelu_coef * (u + 0.044715 * squared * u))
        hidden[rows, :] = (0.5 * u * (1.0 + bent)).astype(BF)
        slope = 0.5 * (1.0 + bent) + 0.5 * u * (1.0 - bent * bent) * gelu_coef * (
            1.0 + 3.0 * 0.044715 * squared
        )
        grad = (mm_nt(cot[rows, :], w_outer[...]) * slope).astype(BF)
        grad_inner[rows, :] = grad
        hidden.push(rows)
        grad_inner.push(rows)
        return mm_nt(grad, w_in[...]), carry

    for out, first_tile in ((keep, 0), (send, half // TILE)):
        for t in range(2):
            rows = pl.ds(t * TILE, TILE)
            out[rows, :] = tile(first_tile + t, 0)[0].astype(BF)
            out.push(rows)
    for copy in copies[arrived:]:
        copy.wait()


def transposed_product(big, left, right, tile=TILE):
    left[0:8, :], right[0:8, :]

    def one(i, carry):
        cols = pl.ds(pl.multiple_of(i * tile, tile), tile)
        big[cols, :] = mm_tn(left[:, cols], right[...])
        return carry

    lax.fori_loop(0, left.shape[1] // tile, one, 0)


def others_of(at):
    za, zl = at[1], at[2]
    return za * 2 + zl, za * 2 + 1 - zl, 2 - 2 * za + zl, 3 - 2 * za - zl


def inner_grad_kernel(at, h2, grad_inner, own, to_l, to_a, to_la, big):
    transposed_product(big, h2, grad_inner)
    n = own.shape[0] // 2
    for t, out in zip(others_of(at), (own, to_l, to_a, to_la)):
        for i in range(2):
            out[pl.ds(i * n, n), :] = big[aligned(i * 4 + t, n), :].astype(out.dtype)


def outer_grad_kernel(at, hidden, cot, w_outer, own, to_l, to_a, to_la, keep, send, big):
    half = keep.shape[0]
    send[...] = mm(hidden[pl.ds(half, half), :], w_outer[...]).astype(BF)
    keep[...] = mm(hidden[pl.ds(0, half), :], w_outer[...])
    transposed_product(big, hidden, cot)
    n = own.shape[0]
    for t, out in zip(others_of(at), (own, to_l, to_a, to_la)):
        out[...] = big[aligned(t, n), :].astype(out.dtype)


def payload_kernel(head_keep, head_got, payload):
    m = head_keep.shape[1] // 4
    for d in range(8):
        rows = pl.ds((d & 3) * m, m)
        payload[d] = (head_keep[d >> 2, rows, :] + head_got[d >> 2, rows, :].astype(F32)).astype(BF)


def last_kernel(
    at, got, near_x, far_x, far_y, query, key, value, sum_a, sum_b, sum_c, sum_d, inner_g
):
    x, y, c = at[0], at[3], at[4]
    per = query.shape[0]
    for w in range(4):
        part = ((near_x, far_x)[w >> 1])[...] if w & 1 == 0 else far_y[w >> 1]
        for s in range(2):
            side = (x ^ (w >> 1)) * 16 + (y ^ (w & 1)) * 2 + (c ^ s)
            for t in range(part.shape[2] // HD):
                inner_g[:, aligned(t * 4 + side, HD)] = part[s, :, t * HD : (t + 1) * HD].astype(F32)
    inner_g.push()
    total = got[0, pl.ds(per, 16), pl.ds(0, HD)].astype(F32)
    for h in range(8):
        for n, out in enumerate((query, key, value)):
            out[:, pl.ds(h * HD, HD)] = got[h, pl.ds(0, per), pl.ds(n * HD, HD)].astype(F32)
        if h:
            total = total + got[h, pl.ds(per, 16), pl.ds(0, HD)].astype(F32)
    for n, out in enumerate((sum_a, sum_b, sum_c, sum_d)):
        out[...] = total[0:1, n * per : (n + 1) * per]


def branch_kernel(at, parts, scaled, inverse, gains, cot, *refs):
    pieces, (grad_middle, branch, go, sums, out_w, sems) = refs[:8], refs[8:]
    copies = place_w_out(at, pieces, out_w, sems)
    rows, width = scaled.shape
    tok = rows // 2
    grad = parts[0].astype(F32)
    for n in range(1, 4):
        grad = grad + parts[n].astype(F32)
    n2 = scaled[...]
    sums[0:1, :] = jnp.sum(grad * n2, 0, keepdims=True)
    sums[1:2, :] = jnp.sum(grad, 0, keepdims=True)
    a = grad * gains[2:3, :]
    grad = inverse[:, 0:1] * (
        a - jnp.mean(a, -1, keepdims=True) - n2 * jnp.mean(a * n2, -1, keepdims=True)
    )
    for s in range(2):
        part = pl.ds(s * tok, tok)
        grad_middle[part, :] = cot[s].astype(F32) + grad[s * tok : (s + 1) * tok]
    grad_middle.push()
    branch[...] = grad_middle[...].astype(BF)
    branch.push()
    for copy in copies:
        copy.wait()
    out = mm_nt(branch[...], out_w[...]).astype(BF)
    for s in range(16):
        head = (s >> 3) * 4 + (s & 3)
        seq = s >> 2 & 1
        go[s] = out[seq * tok : (seq + 1) * tok, head * HD : (head + 1) * HD]


def fine_backward_kernel(at, query, own, other, go_ref, out_f, lse_ref, gq_ref, keep, send, acc):
    rows_all = query.shape[0]
    tiles = rows_all // TILE
    c = at[4]
    both = (own, other)
    keep[...] = jnp.zeros(keep.shape, keep.dtype)
    acc[...] = jnp.zeros_like(acc)
    totals = (keep, acc)

    def tile(t, carry):
        rows = aligned(t, TILE)
        q = query[rows, :]
        go = go_ref[pl.ds(t * (TILE // 64), TILE // 64)].reshape(TILE, HD)
        delta = jnp.sum(go.astype(F32) * out_f[rows, :], -1, keepdims=True)
        lse = lse_ref[rows, 0:1]

        def one(u, gq, masked):
            cols = aligned(u, TILE)
            for n in range(2):
                kk = both[n][cols, pl.ds(0, HD)]
                p = jnp.exp(mm_nt(q, kk) * SCALE - lse)
                if masked:
                    p = jnp.where(causal(c, c if n == 0 else 1 - c), p, 0.0)
                totals[n][cols, pl.ds(HD, HD)] += mm_tn(p.astype(BF), go)
                ds = (p * (mm_nt(go, both[n][cols, pl.ds(HD, HD)]) - delta)).astype(BF)
                totals[n][cols, pl.ds(0, HD)] += mm_tn(ds, q)
                gq = gq + mm(ds, kk)
            return gq

        gq = jnp.zeros((TILE, HD), F32)
        for u in range(t + 1):
            gq = one(u, gq, u == t)
        gq_ref[rows, :] = (gq * SCALE).astype(BF)
        gq_ref.push(rows)
        return carry

    for t in range(tiles):
        tile(t, 0)
    send[:, :HD] = (acc[:, :HD] * SCALE).astype(BF)
    send[:, HD:] = acc[:, HD:].astype(BF)
    send.push()
    keep[:, :HD] = keep[:, :HD] * SCALE


def partial_kernel(at, *refs):
    blocks, (gq, keep, got, weights) = refs[:8], refs[8:12]
    grads, parts, sums, tokens, sems = refs[12:]
    x, za, zl, y = (at[i] for i in range(4))
    copies = []
    for n in range(8):
        for s in range(2):
            j = (x ^ (n >> 2)) * 8 + (za ^ s) * 4 + (zl ^ (n >> 1 & 1)) * 2 + (y ^ (n & 1))
            copies.append(
                pltpu.make_async_copy(
                    blocks[n].at[s], tokens.at[aligned(j, 64), :], sems.at[len(copies)]
                )
            )
            copies[-1].start()
    for copy in copies:
        copy.wait()
    tiles = gq.shape[0] // TILE
    for t in range(tiles):
        rows = pl.ds(t * TILE, TILE)
        grads[rows, pl.ds(0, HD)] = gq[rows, :]
        grads[rows, pl.ds(HD, 2 * HD)] = (keep[rows, :] + got[rows, :].astype(F32)).astype(BF)
        part = mm_nt(grads[rows, :], weights[...])
        normed, _ = norm_of(tokens[rows, :].astype(F32))
        one = jnp.sum(part * normed, 0, keepdims=True)
        two = jnp.sum(part, 0, keepdims=True)
        if t == 0:
            sums[0:1, :] = one
            sums[1:2, :] = two
        else:
            sums[0:1, :] += one
            sums[1:2, :] += two
        for i in range(4):
            parts[(t >> 1) * 4 + i, za ^ (t & 1)] = part[i * 64 : (i + 1) * 64].astype(BF)
        grads.push(rows)
        if t & 1:
            parts.push(pl.ds((t >> 1) * 4, 4))


def total_kernel(parts, keep, send):
    total = parts[0, 0].astype(F32)
    other = parts[0, 1].astype(F32)
    for n in range(1, 8):
        total = total + parts[n, 0].astype(F32)
        other = other + parts[n, 1].astype(F32)
    keep[...] = total
    send[...] = other.astype(BF)


def head_grad_kernel(at, left, right, sums, keep, send, big):
    c = at[4]
    per = left.shape[1] // 32
    transposed_product(big, left, right)
    spare = keep.shape[2] - sums.shape[1]
    for q in range(16):
        keep[q, pl.ds(0, per), :] = big[aligned(2 * q + c, per), :]
        send[q, pl.ds(0, per), :] = big[aligned(2 * q + 1 - c, per), :].astype(BF)
    pad = jnp.zeros((16, spare), F32)
    for q in range(16):
        pair = jnp.concatenate([sums[2 * q : 2 * q + 2, :], pad[:2]], 1)
        mine = jnp.where(c == 0, pair[0:1], pair[1:2])
        other = jnp.where(c == 0, pair[1:2], pair[0:1])
        keep[q, pl.ds(per, 16), :] = jnp.broadcast_to(mine, (16, keep.shape[2]))
        send[q, pl.ds(per, 16), :] = jnp.broadcast_to(other, (16, keep.shape[2])).astype(BF)


def core_grad_kernel(at, left, right, keep, send, big):
    c = at[4]
    per = left.shape[1] // 32
    transposed_product(big, left, right)
    for q in range(16):
        rows = pl.ds(q * per, per)
        keep[rows, :] = big[aligned(2 * q + c, per), :]
        send[rows, :] = big[aligned(2 * q + 1 - c, per), :].astype(BF)


def input_kernel(at, keep, got, tokens, grad_middle, gains, grad_tokens):
    za = at[1]
    tok = tokens.shape[1]
    for n in range(2):
        seq = za if n == 0 else 1 - za
        part = keep[...] if n == 0 else got[...].astype(F32)
        n1, inv = norm_of(tokens[seq].astype(F32))
        a = part * gains[0:1, :]
        grad_tokens[seq] = grad_middle[aligned(seq, tok), :] + inv * (
            a - jnp.mean(a, -1, keepdims=True) - n1 * jnp.mean(a * n1, -1, keepdims=True)
        )


def far_kernel(keep, got, own, on_z, on_y, far_a, far_b):
    n = own.shape[0]
    for i, out in enumerate((own, on_z, on_y)):
        rows = pl.ds(i * n, n)
        out[...] = keep[rows, :] + got[rows, :].astype(F32)
    for i, out in enumerate((far_a, far_b)):
        rows = pl.ds(3 * n + i * (n // 2), n // 2)
        out[...] = (keep[rows, :] + got[rows, :].astype(F32)).astype(BF)


def near_kernel(on_z, on_y, got_a, got_b, send_z, send_y):
    n = got_a.shape[0]
    first, second = pl.ds(0, n), pl.ds(n, n)
    send_z[first, :] = (on_z[first, :] + got_a[...].astype(F32)).astype(BF)
    send_z[second, :] = on_z[second, :].astype(BF)
    send_y[first, :] = on_y[first, :].astype(BF)
    send_y[second, :] = (on_y[second, :] + got_b[...].astype(F32)).astype(BF)


def result_sum_kernel(middle, own, got_z, got_y, out):
    out[...] = (
        middle[...] + own[...] + got_z[...].astype(F32) + got_y[...].astype(F32)
    ).astype(BF)


def fold_kernel(at, keep, got, parts):
    x, y = at[0], at[3]
    rows = parts.shape[1]
    for n in range(4):
        here = pl.ds(n * rows, rows)
        z = x ^ (1 if n in (1, 3) else 0)
        w = y ^ (1 if n in (2, 3) else 0)
        parts[z * 2 + w] = (keep[here, :].astype(F32) + got[here, :].astype(F32)).astype(BF)


def stage(*values):
    return lax.optimization_barrier(values)


def grow(v, axis):
    return jnp.concatenate([v, swap(v, axis)], 0)


def half_swap(v, axis):
    return swap(pick(v, 1 - lax.axis_index(axis)), axis)


def fine_layer(
    tokens,
    cotangent,
    ln1_gain,
    ln1_bias,
    w_query,
    w_key,
    w_value,
    w_out,
    ln2_gain,
    ln2_bias,
    w_inner,
    w_outer,
):
    seqs, tok, width = tokens.shape
    rows = seqs * tok
    half = rows // 2
    per = w_query.shape[0]
    unit = w_outer.shape[0]
    hidden_units = 4 * unit
    all_rows = 8 * rows
    coords = jnp.stack([lax.axis_index(a) for a in ("x", "za", "zl", "y", "c")]).astype(jnp.int32)
    x, za = lax.axis_index("x"), lax.axis_index("za")
    cube, owners = ("x", "zl", "y"), ("x", "za", "zl", "y")
    cot = cotangent.reshape(rows, width)

    def split(axis, keep, got, shape):
        keep, got = keep.reshape(shape), got.reshape(shape)
        i = lax.axis_index(axis)
        mine = pick(keep, i, 1) + pick(got, i, 1).astype(F32)
        return mine, (pick(keep, 1 - i, 1) + pick(got, 1 - i, 1).astype(F32)).astype(BF)

    head_w, inner_w = call(
        pack_kernel,
        [((16, 3 * per + 16, HD), BF), ((8, per, hidden_units), BF)],
        [w_query, w_key, w_value]
        + [g.reshape(1, per) for g in (ln1_gain, ln1_bias, ln2_gain, ln2_bias)]
        + [w_inner],
        name="pack",
    )
    moved, head_w, inner_w, w_out, w_outer = stage(
        swap(pick(tokens, 1 - za), "za"), head_w, inner_w, w_out, w_outer
    )
    block = jnp.stack([pick(tokens, za), moved])
    on_x, on_z, on_y, head_w = stage(
        swap(block, "x"), swap(block, "zl"), swap(block, "y"), head_w
    )
    on_xz, on_xy, on_zy, on_xyz, head_w, w_out_z = stage(
        swap(on_x, "zl"),
        swap(on_y, "x"),
        swap(on_z, "y"),
        lax.ppermute(block, cube, [(i, 7 - i) for i in range(8)]),
        lax.all_to_all(head_w, owners, 0, 0, tiled=True),
        swap(after(w_out, on_x), "za"),
    )
    head_c, w_outer, inner_w, w_out_z = stage(swap(head_w, "c"), w_outer, inner_w, w_out_z)
    blocks = [block, on_y, on_z, on_zy, on_x, on_xy, on_xz, on_xyz]
    out_w = jnp.stack([w_out, w_out_z])
    h1, query, kv, gains, head_w = call(
        qkv_kernel,
        [
            ((16 * tok, width), BF),
            ((16 * tok, HD), BF),
            ((16 * tok, 2 * HD), BF),
            ((8, width), F32),
            ((width, 3 * HD), BF),
        ],
        blocks + [head_w, head_c],
        coords,
        name="qkv",
    )
    kv, query, out_x, outer_a, outer_l, inner_w = stage(
        kv,
        query,
        swap(out_w, "x"),
        swap(w_outer, "za"),
        swap(w_outer, "zl"),
        lax.all_to_all(inner_w, ("x", "y", "c"), 0, 0, tiled=True),
    )
    out_w = jnp.concatenate([out_w, out_x], 0)
    kv_other, out_w, inner_w = stage(swap(kv, "c"), out_w, inner_w)
    out, out_f, lse, query, kv, kv_other = call(
        fine_forward_kernel,
        [((16, tok, HD), BF), ((16 * tok, HD), F32), ((16 * tok, HD), F32)],
        [query, kv, kv_other],
        coords,
        save=(0, 1, 2),
        scratch=[pltpu.VMEM((2 * 16 * tok // TILE, TILE, TILE), F32)],
        name="attention_forward",
    )
    out, out_z, out_y, inner_a, inner_l, cot = stage(
        out,
        swap(out_w, "zl"),
        swap(out_w, "y"),
        swap(inner_w, "za"),
        swap(inner_w, "zl"),
        cot,
    )
    mixed, cot_z, cot_y, cot_c, out_zy, outer_la, inner_la, *out_c = stage(
        lax.all_to_all(out, owners, 0, 0, tiled=True),
        swap(cot, "x"),
        swap(cot, "y"),
        swap(cot, "c"),
        swap(out_z, "y"),
        swap(outer_a, "zl"),
        swap(inner_a, "zl"),
        swap(out_w, "c"),
        swap(out_z, "c"),
        swap(out_y, "c"),
    )
    (out_zyc,) = stage(swap(out_zy, "c"))
    pieces = [out_w, out_z, out_y, out_zy] + out_c + [out_zyc]
    mixed, middle, scaled, inverse, h2 = call(
        middle_kernel,
        [
            ((rows, width), BF),
            ((rows, width), F32),
            ((rows, width), F32),
            ((rows, HD), F32),
            ((rows, width), BF),
        ],
        [mixed, tokens, gains] + pieces,
        coords,
        raw=range(3, 11),
        scratch=[pltpu.VMEM((width, width), BF), pltpu.SemaphoreType.DMA((32,))],
        name="middle",
    )
    cot_z, cot_y = after(cot_z, h2), after(cot_y, h2)
    h2_z, h2_y, h2_c, cot_a, cot_b, cot_zc, cot_yc = stage(
        swap(h2, "x"),
        swap(h2, "y"),
        swap(h2, "c"),
        swap(cot_z[:half], "y"),
        swap(cot_y[half:], "x"),
        swap(cot_z, "c"),
        swap(cot_y, "c"),
    )
    h2_a, h2_b, h2_zc, h2_yc, cot_ac, cot_bc = stage(
        swap(h2_z[:half], "y"),
        swap(h2_y[half:], "x"),
        swap(h2_z, "c"),
        swap(h2_y, "c"),
        swap(cot_a, "c"),
        swap(cot_b, "c"),
    )
    h2_ac, h2_bc = stage(swap(h2_a, "c"), swap(h2_b, "c"))
    h2_all, cot_all, outer_w, hidden, grad_inner, keep, send = call(
        inner_kernel,
        [
            ((all_rows, width), BF, "raw"),
            ((all_rows, width), BF, "raw"),
            ((hidden_units, width), BF, "raw"),
            ((all_rows, hidden_units), BF),
            ((all_rows, hidden_units), BF),
            ((all_rows // 2, width), BF),
            ((all_rows // 2, width), BF),
        ],
        [h2, h2_z, h2_y, h2_a, h2_b, h2_c, h2_zc, h2_yc, h2_ac, h2_bc]
        + [cot, cot_z, cot_y, cot_a, cot_b, cot_c, cot_zc, cot_yc, cot_ac, cot_bc]
        + [p.reshape(2, 4 * per, hidden_units) for p in (inner_w, inner_l, inner_a, inner_la)]
        + [w_outer, outer_l, outer_a, outer_la],
        coords,
        raw=range(10, 28),
        scratch=[
            pltpu.VMEM((all_rows, width), BF),
            pltpu.VMEM((all_rows, width), BF),
            pltpu.VMEM((width, hidden_units), BF),
            pltpu.VMEM((hidden_units, width), BF),
            pltpu.SemaphoreType.DMA((25,)),
        ],
        name="inner",
    )

    (got,) = stage(swap(send, "c"))
    (parts,) = call(
        fold_kernel, [((4, rows, width), BF)], [keep, got], coords, name="fold"
    )
    n_in, n_out = 8 * per, unit
    inner_g, in_l, in_a, in_la = call(
        inner_grad_kernel,
        [((n_in, hidden_units), F32)] + [((n_in, hidden_units), BF)] * 3,
        [h2_all, grad_inner],
        coords,
        scratch=[pltpu.VMEM((width, hidden_units), F32)],
        name="inner_grad",
    )
    parts, inner_g, in_l, in_a, in_la = stage(parts, inner_g, in_l, in_a, in_la)
    outer_g, outer_l, outer_a, outer_la, res_keep, res_send = call(
        outer_grad_kernel,
        [((n_out, width), F32)]
        + [((n_out, width), BF)] * 3
        + [((all_rows // 2, width), F32), ((all_rows // 2, width), BF)],
        [after(hidden, in_l), cot_all, outer_w],
        coords,
        scratch=[pltpu.VMEM((hidden_units, width), F32)],
        name="outer_grad",
    )
    parts, in_l, in_a, outer_g, outer_l, outer_a, outer_la, res_keep, res_send, in_la = stage(
        lax.all_to_all(parts, ("x", "y"), 0, 0, tiled=True),
        swap(in_l, "zl"),
        swap(in_a, "za"),
        outer_g,
        outer_l,
        outer_a,
        outer_la,
        res_keep,
        res_send,
        in_la,
    )
    grad_middle, branch, go, sums_two = call(
        branch_kernel,
        [
            ((rows, width), F32),
            ((rows, width), BF),
            ((16, tok, HD), BF),
            ((2, width), F32),
        ],
        [parts, scaled, inverse, gains, cotangent] + pieces,
        coords,
        raw=range(5, 13),
        scratch=[pltpu.VMEM((width, width), BF), pltpu.SemaphoreType.DMA((32,))],
        name="branch",
    )
    go, branch, res_got, outer_l, outer_a = stage(
        go, branch, swap(res_send, "c"), outer_l, outer_a
    )
    res = (res_keep + res_got.astype(F32)).reshape(4, rows, width)
    far_a, far_b = res[3, :half].astype(BF), res[3, half:].astype(BF)
    out_keep, out_send = call(
        core_grad_kernel,
        [((width // 2, width), F32), ((width // 2, width), BF)],
        [mixed, branch],
        coords,
        scratch=[pltpu.VMEM((width, width), F32)],
        name="out_grad",
    )
    diagonal = [(i, 3 - i) for i in range(4)]
    go, outer_l, outer_a, in_la, outer_la, out_keep, out_send, res, far_a, far_b = stage(
        lax.all_to_all(go, owners, 0, 0, tiled=True),
        swap(outer_l, "zl"),
        swap(outer_a, "za"),
        in_la,
        outer_la,
        out_keep,
        out_send,
        res,
        far_a,
        far_b,
    )
    gq, keep, send = call(
        fine_backward_kernel,
        [((16 * tok, HD), BF), ((16 * tok, 2 * HD), F32), ((16 * tok, 2 * HD), BF)],
        [query, kv, kv_other, go, out_f, lse],
        coords,
        scratch=[pltpu.VMEM((16 * tok, 2 * HD), F32)],
        name="attention_backward",
    )
    gq, keep, send, got_a, got_b, out_got, in_la = stage(
        gq,
        keep,
        send,
        swap(far_a, "y"),
        swap(far_b, "x"),
        swap(out_send, "c"),
        lax.ppermute(in_la, ("za", "zl"), diagonal),
    )
    out_keep, out_send = split("x", out_keep, out_got, (1, 2, 8 * per, width))
    got, out_keep, out_send, outer_la = stage(swap(send, "c"), out_keep, out_send, outer_la)
    grads, parts, sums = call(
        partial_kernel,
        [
            ((16 * tok, 3 * HD), BF),
            ((8, 2, tok, width), BF),
            ((2, width), F32),
        ],
        blocks + [gq, keep, got, head_w],
        coords,
        raw=range(8),
        scratch=[pltpu.VMEM((16 * tok, width), BF), pltpu.SemaphoreType.DMA((16,))],
        name="partial",
    )
    grads, parts, sums, out_keep, out_got, outer_la = stage(
        grads,
        parts,
        sums,
        out_keep,
        swap(out_send, "x"),
        lax.ppermute(outer_la, ("za", "zl"), diagonal),
    )
    parts = lax.all_to_all(parts, cube, 0, 0, tiled=True)
    sums = jnp.concatenate([sums, sums_two], 0)
    sums = sums.reshape(4, 32, per).transpose(1, 0, 2).reshape(32, 4 * per)
    head_keep, head_send = call(
        head_grad_kernel,
        [((16, per + 16, 3 * HD), F32), ((16, per + 16, 3 * HD), BF)],
        [h1, grads, sums],
        coords,
        scratch=[pltpu.VMEM((width, 3 * HD), F32)],
        name="head_grad",
    )
    head_keep, head_send = stage(head_keep, head_send)
    out_keep, out_send = split(
        "y", out_keep, after(out_got, head_send), (4, 2, per, width)
    )
    inner_g = inner_g + after(in_l, head_send).astype(F32) + in_a.astype(F32) + in_la.astype(F32)
    inner_g = inner_g.astype(BF).reshape(4, 2, per, hidden_units)
    got_a = after(got_a, head_send)
    res_z = jnp.concatenate([res[1, :half] + got_a.astype(F32), res[1, half:]], 0).astype(BF)
    res_y = jnp.concatenate([res[2, :half], res[2, half:] + got_b.astype(F32)], 0).astype(BF)
    inner_own = pick(inner_g, lax.axis_index("c"), 1)
    inner_send = pick(inner_g, 1 - lax.axis_index("c"), 1)
    head_keep, head_got, out_keep, out_send, inner_own, inner_send, res_z, res_y = stage(
        head_keep, swap(head_send, "c"), out_keep, out_send, inner_own, inner_send, res_z, res_y
    )
    head_keep, head_send = split("za", head_keep, head_got, (2, 2, 4 * (per + 16), 3 * HD))
    head_keep, head_send, out_send = stage(head_keep, head_send, out_send)
    outer_g = (
        outer_g
        + after(outer_l, head_send).astype(F32)
        + outer_a.astype(F32)
        + outer_la.astype(F32)
    )
    head_keep, head_got, out_keep, out_got, inner_got, got_z, res_y, outer_g = stage(
        head_keep,
        swap(head_send, "za"),
        out_keep,
        swap(out_send, "y"),
        swap(inner_send, "c"),
        swap(res_z, "x"),
        res_y,
        outer_g,
    )
    inner_g = jnp.stack([inner_own, inner_got]).reshape(2, 2, 2, per, hidden_units)
    x = lax.axis_index("x")
    near_x, inner_send = pick(inner_g, x, 1), pick(inner_g, 1 - x, 1)
    (payload,) = call(
        payload_kernel,
        [((8, per + 16, 3 * HD), BF)],
        [head_keep, head_got],
        name="payload",
    )
    out_keep, out_send = split("za", out_keep, out_got, (1, 2, 2 * per, width))
    parts, payload, near_x, inner_send, out_keep, out_send = stage(
        parts, payload, near_x, inner_send, out_keep, out_send
    )
    payload = lax.all_to_all(payload, cube, 0, 0, tiled=True)
    total, send = call(
        total_kernel, [((tok, width), F32), ((tok, width), BF)], [parts], name="total"
    )
    total, send, near_x, inner_send, out_send, res_y = stage(
        total, send, near_x, inner_send, out_send, res_y
    )
    got, out_send, got_y, far_x, near_x = stage(
        swap(send, "za"),
        out_send,
        swap(res_y, "y"),
        swap(inner_send, "x"),
        near_x,
    )
    y = lax.axis_index("y")
    inner_send = jnp.stack([pick(near_x, 1 - y, 1), pick(far_x, 1 - y, 1)])
    near_x, far_x = pick(near_x, y, 1), pick(far_x, y, 1)
    (grad_tokens,) = call(
        input_kernel,
        [((seqs, tok, width), F32)],
        [total, got, tokens, grad_middle, gains],
        coords,
        name="input",
    )
    result = (
        middle + res[0] + after(got_z, got).astype(F32) + got_y.astype(F32)
    ).astype(BF)
    payload, out_got, grad_tokens, result, far_y, near_x, far_x = stage(
        payload,
        swap(out_send, "za"),
        grad_tokens,
        result,
        swap(inner_send, "y"),
        near_x,
        far_x,
    )
    out_keep, out_send = split("zl", out_keep, out_got, (1, 2, per, width))
    out_keep, out_send = stage(out_keep, out_send)
    query_g, key_g, value_g, *sums, inner_g = call(
        last_kernel,
        [((per, width), F32)] * 3
        + [((1, per), F32)] * 4
        + [((per, 8 * hidden_units), F32)],
        [payload, near_x, far_x, far_y],
        coords,
        name="last",
    )
    query_g, key_g, value_g, inner_g, out_got, result, *sums = stage(
        query_g, key_g, value_g, inner_g, swap(out_send, "zl"), result, *sums
    )
    sums = [v.reshape(per) for v in sums]
    return (
        result.reshape(seqs, tok, width),
        grad_tokens,
        sums[0],
        sums[1],
        query_g,
        key_g,
        value_g,
        out_keep[0] + out_got[0].astype(F32),
        sums[2],
        sums[3],
        inner_g,
        outer_g,
    )


def solution(mesh):
    blocks = mesh.shape["blk"]
    if blocks == 16:
        sizes = (2, 2, 1, 2, 2, 2)
        roles = (True, "za", ("x", "zl", "y"), ("c",), ("x", "za", "zl", "y"))
    else:
        sizes = (2, 8, blocks // 64, 2, 2, 2)
        roles = (False, "x", ("za",), ("zb", "zl", "y", "c"), ("x", "za"))
    fine = Mesh(mesh.devices.reshape(sizes), AXES)
    tok, row, vec = P(None, AXES, None), P(AXES, None), P(AXES)
    in_specs = (tok, tok, vec, vec, row, row, row, row, vec, vec, row, row)
    out_specs = (tok, tok, vec, vec, row, row, row, row, vec, vec, row, row)
    return jax.shard_map(
        fine_layer if blocks == 16 else functools.partial(on_device, roles),
        mesh=fine,
        in_specs=in_specs,
        out_specs=out_specs,
        check_vma=False,
    )
```

profile of v0, /device:TPU:0, one launch (start us, length us, event | category | flops | bytes accessed | tf_op | source)
XLA Modules:
  0.0 311.4 jit_solution(6966324464207729366)
XLA Ops:
  1.7 4.1 %collective-permute-start = (bf16[64,1024]{1,0:T(8,128)(2,1)S(1)}, bf16[64,1024]{1,0:T(8,128)(2,1)S(1)}, u32[]{:S(2)}, u32[]{:S(2)}) collective-permute-start(bf16[64,1024]{1,0:T(8,128)(2,1)S(1)} %get-tuple-element.491), channel_id=1, source_target_pairs={{0,8},{8,0},{1,9},{9,1},{2,10},{10,2},{3,11},{11,3},{4,12},{12,4},... | collective-permute-start | bytes 393224 | tf_op jit(solution)/shard_map/ppermute | solution.py:51
  7.9 4.2 %collective-permute-done = bf16[64,1024]{1,0:T(8,128)(2,1)S(1)} collective-permute-done((bf16[64,1024]{1,0:T(8,128)(2,1)S(1)}, bf16[64,1024]{1,0:T(8,128)(2,1)S(1)}, u32[]{:S(2)}, u32[]{:S(2)}) %collective-permute-start) | collective-permute-done | bytes 131104 | tf_op jit(solution)/shard_map/ppermute | solution.py:51
  22.1 5.7 %all-to-all-start = ((bf16[16,112,128]{2,1,0:T(8,128)(2,1)}), bf16[16,112,128]{2,1,0:T(8,128)(2,1)S(1)}, u32[]{:S(2)}, u32[]{:S(2)}) async-start(bf16[16,112,128]{2,1,0:T(8,128)(2,1)} %get-tuple-element.248), calls=%async_computation | async-start | bytes 917504 | tf_op jit(solution)/shard_map/all_to_all | solution.py:1168
  35.6 11.4 %collective-permute-done.7.refs_8_ = bf16[2,64,1024]{2,1,0:T(8,128)(2,1)S(1)} collective-permute-done((bf16[2,64,1024]{2,1,0:T(8,128)(2,1)S(1)}, bf16[2,64,1024]{2,1,0:T(8,128)(2,1)S(1)}, u32[]{:S(2)}, u32[]{:S(2)}) %collective-permute-start.7) | collective-permute-done | bytes 262176 | tf_op jit(solution)/shard_map/ppermute | solution.py:1167
  60.3 7.2 %qkv.1 = (bf16[1024,1024]{1,0:T(8,128)(2,1)}, bf16[1024,128]{1,0:T(8,128)(2,1)}, bf16[1024,256]{1,0:T(8,128)(2,1)}, f32[8,1024]{1,0:T(8,128)}, bf16[1024,384]{1,0:T(8,128)(2,1)}) custom-call(s32[5]{0:T(128)} %stack.57.refs_0_, bf16[2,64,1024]{2,1,0:T(8,128)(2,1)} %copy-done.1, bf16[2,64,1024]{2,1,0:T(8,128)(2,1)} %copy-done.10, ...), custom_call_target="tpu_custom_call" | custom-call | tf_op jit(solution)/shard_map/qkv/pallas_call | solution.py:603
  75.5 6.0 %attention_forward.1 = (bf16[16,64,128]{2,1,0:T(8,128)(2,1)}, f32[1024,128]{1,0:T(8,128)}, f32[1024,128]{1,0:T(8,128)}, bf16[1024,128]{1,0:T(8,128)(2,1)}, bf16[...) custom-call(s32[5]{0:T(128)} %stack.57.refs_0_, bf16[1024,128]{1,0:T(8,128)(2,1)} %get-tuple-element.265.refs_1_, ...), custom_call_target="tpu_custom_call" | custom-call | tf_op jit(solution)/shard_map/attention_forward/pallas_call | solution.py:603
  92.1 4.7 %all-to-all-start.2 = ((bf16[16,64,128]{2,1,0:T(8,128)(2,1)}), bf16[16,64,128]{2,1,0:T(8,128)(2,1)S(1)}, u32[]{:S(2)}, u32[]{:S(2)}) async-start(bf16[16,64,128]{2,1,0:T(8,128)(2,1)} %get-tuple-element.276), calls=%async_computation.2 | async-start | bytes 524288 | tf_op jit(solution)/shard_map/all_to_all | solution.py:1215
  100.6 7.3 %collective-permute-done.21.refs_7_.refs_9_ = bf16[4,32,1024]{2,1,0:T(8,128)(2,1)S(1)} collective-permute-done((bf16[4,32,1024]{2,1,0:T(8,128)(2,1)S(1)}, bf16[4,32,1024]{2,1,0:T(8,128)(2,1)S(1)}, u32[]{:S(2)}, u32[]{:S(2)}) %collective-permute-start.21) | collective-permute-done | bytes 262176 | tf_op jit(solution)/shard_map/ppermute | solution.py:51
  111.7 4.6 %middle.1 = (bf16[128,1024]{1,0:T(8,128)(2,1)}, f32[128,1024]{1,0:T(8,128)}, f32[128,1024]{1,0:T(8,128)}, f32[128,128]{1,0:T(8,128)}, bf16[128,1024]{1,0:T(8,128)(2,1)}) custom-call(s32[5]{0:T(128)} %stack.57.refs_0_, bf16[16,64,128]{2,1,0:T(8,128)(2,1)} %copy-done.23, bf16[2,64,1024]{2,1,0:T(8,128)(2,1)} %refs_3_.1, ...), custom_call_target="tpu_custom_call" | custom-call | tf_op jit(solution)/shard_map/middle/pallas_call | solution.py:603
  123.2 4.9 %collective-permute-done.28.refs_2_ = bf16[128,1024]{1,0:T(8,128)(2,1)S(1)} collective-permute-done((bf16[128,1024]{1,0:T(8,128)(2,1)}, bf16[128,1024]{1,0:T(8,128)(2,1)S(1)}, u32[]{:S(2)}, u32[]{:S(2)}) %collective-permute-start.28) | collective-permute-done | bytes 262176 | tf_op jit(solution)/shard_map/ppermute | solution.py:51
  139.3 9.3 %inner.1 = (bf16[1024,1024]{1,0:T(8,128)(2,1)}, bf16[1024,1024]{1,0:T(8,128)(2,1)}, bf16[512,1024]{1,0:T(8,128)(2,1)}, bf16[1024,512]{1,0:T(8,128)(2,1)}, bf16[1...) custom-call(s32[5]{0:T(128)} %stack.57.refs_0_, ...), custom_call_target="tpu_custom_call" | custom-call | tf_op jit(solution)/shard_map/inner/pallas_call | solution.py:603
  148.9 5.7 %inner_grad.1 = (f32[256,512]{1,0:T(8,128)}, bf16[256,512]{1,0:T(8,128)(2,1)}, bf16[256,512]{1,0:T(8,128)(2,1)}, bf16[256,512]{1,0:T(8,128)(2,1)}) custom-call(s32[5]{0:T(128)} %stack.57.refs_0_, bf16[1024,1024]{1,0:T(8,128)(2,1)} %get-tuple-element.315.refs_1_, bf16[1024,512]{1,0:T(8,128)(2,1)} %get-tuple-element.316.refs_2_), custom_call_target="tpu_custom_call" | custom-call | tf_op jit(solution)/shard_map/inner_grad/pallas_call | solution.py:603
  165.6 7.9 %outer_grad.1 = (f32[128,1024]{1,0:T(8,128)}, bf16[128,1024]{1,0:T(8,128)(2,1)}, bf16[128,1024]{1,0:T(8,128)(2,1)}, bf16[128,1024]{1,0:T(8,128)(2,1)}, f32[512,1024]{1,0:T(8,128)}, /*index=5*/bf16[512,1024]{1,0:T(8,128)(2,1)}) custom-call(s32[5]{0:T(128)} %stack.57.refs_0_, bf16[1024,512]{1,0:T(8,128)(2,1)} %get-tuple-element.325.refs_1_, ...), custom_call_target="tpu_custom_call" | custom-call | tf_op jit(solution)/shard_map/outer_grad/pallas_call | solution.py:603
  178.6 5.3 %branch.1 = (f32[128,1024]{1,0:T(8,128)}, bf16[128,1024]{1,0:T(8,128)(2,1)}, bf16[16,64,128]{2,1,0:T(8,128)(2,1)}, f32[2,1024]{1,0:T(2,128)}) custom-call(s32[5]{0:T(128)} %stack.57.refs_0_, bf16[4,128,1024]{2,1,0:T(8,128)(2,1)} %copy-done, f32[128,1024]{1,0:T(8,128)} %get-tuple-element.336.refs_2_, f32[128,128]{1,0:T(8,128)} %get-tuple-element.337.refs_3_, ...), custom_call_target="tpu_custom_call" | custom-call | tf_op jit(solution)/shard_map/branch/pallas_call | solution.py:603
  188.2 3.9 %all-to-all-start.4 = ((bf16[16,64,128]{2,1,0:T(8,128)(2,1)}), bf16[16,64,128]{2,1,0:T(8,128)(2,1)S(1)}, u32[]{:S(2)}, u32[]{:S(2)}) async-start(bf16[16,64,128]{2,1,0:T(8,128)(2,1)} %get-tuple-element.343), calls=%async_computation.4 | async-start | bytes 524288 | tf_op jit(solution)/shard_map/all_to_all | solution.py:1354
  194.2 5.0 %out_grad.1 = (f32[512,1024]{1,0:T(8,128)}, bf16[512,1024]{1,0:T(8,128)(2,1)}) custom-call(s32[5]{0:T(128)} %stack.57.refs_0_, bf16[128,1024]{1,0:T(8,128)(2,1)} %get-tuple-element.348.refs_1_, bf16[128,1024]{1,0:T(8,128)(2,1)} %get-tuple-element.349.refs_2_), custom_call_target="tpu_custom_call" | custom-call | tf_op jit(solution)/shard_map/out_grad/pallas_call | solution.py:603
  202.3 4.6 %all-to-all-done.4.refs_4_ = bf16[16,64,128]{2,1,0:T(8,128)(2,1)S(1)} async-done(((bf16[16,64,128]{2,1,0:T(8,128)(2,1)}), bf16[16,64,128]{2,1,0:T(8,128)(2,1)S(1)}, u32[]{:S(2)}, u32[]{:S(2)}) %all-to-all-start.4) | async-done | bytes 262176 | tf_op jit(solution)/shard_map/all_to_all | solution.py:1354
  210.6 10.6 %attention_backward.1 = (bf16[1024,128]{1,0:T(8,128)(2,1)}, f32[1024,256]{1,0:T(8,128)}, bf16[1024,256]{1,0:T(8,128)(2,1)}) custom-call(s32[5]{0:T(128)} %stack.57.refs_0_, bf16[1024,128]{1,0:T(8,128)(2,1)} %get-tuple-element.270.refs_1_, bf16[1024,256]{1,0:T(8,128)(2,1)} %get-tuple-element.271.refs_2_, bf16[1024,256]{1,0:T(8,128)(2,1)} %get-tuple-element.272.refs_3_, ...), custom_call_target="tpu_custom_call" | custom-call | tf_op jit(solution)/shard_map/attention_backward/pallas_call | solution.py:603
  228.0 6.3 %partial.1 = (bf16[1024,384]{1,0:T(8,128)(2,1)}, bf16[8,2,64,1024]{3,2,1,0:T(8,128)(2,1)}, f32[2,1024]{1,0:T(2,128)}) custom-call(s32[5]{0:T(128)} %stack.57.refs_0_, bf16[2,64,1024]{2,1,0:T(8,128)(2,1)} %copy-done.1, bf16[2,64,1024]{2,1,0:T(8,128)(2,1)} %copy-done.10, bf16[2,64,1024]{2,1,0:T(8,128)(2,1)} %copy-done.9, bf16[2,64,1024]{2,1,0:T(8,128)(2,1)} %copy-done.14, ...), custom_call_target="tpu_custom_call" | custom-call | tf_op jit(solution)/shard_map/partial/pallas_call | solution.py:603
  239.6 4.6 %all-to-all-start.5 = ((bf16[8,2,64,1024]{3,2,1,0:T(8,128)(2,1)}), bf16[8,2,64,1024]{3,2,1,0:T(8,128)(2,1)}, u32[]{:S(2)}, u32[]{:S(2)}) async-start(bf16[8,2,64,1024]{3,2,1,0:T(8,128)(2,1)} %get-tuple-element.378), calls=%async_computation.5 | async-start | bytes 4194304 | tf_op jit(solution)/shard_map/all_to_all | solution.py:1405
  245.8 5.9 %head_grad.1 = (f32[16,48,384]{2,1,0:T(8,128)}, bf16[16,48,384]{2,1,0:T(8,128)(2,1)}) custom-call(s32[5]{0:T(128)} %stack.57.refs_0_, bf16[1024,1024]{1,0:T(8,128)(2,1)} %get-tuple-element.379.refs_1_, bf16[1024,384]{1,0:T(8,128)(2,1)} %get-tuple-element.380.refs_2_, f32[32,128]{1,0:T(8,128)} %reshape.313.refs_3_), custom_call_target="tpu_custom_call" | custom-call | tf_op jit(solution)/shard_map/head_grad/pallas_call | solution.py:603
  262.5 9.2 %collective-permute-done.58 = bf16[4,32,1024]{2,1,0:T(8,128)(2,1)S(1)} collective-permute-done((bf16[4,32,1024]{2,1,0:T(8,128)(2,1)S(1)}, bf16[4,32,1024]{2,1,0:T(8,128)(2,1)S(1)}, u32[]{:S(2)}, u32[]{:S(2)}) %collective-permute-start.58) | collective-permute-done | bytes 262176 | tf_op jit(solution)/shard_map/ppermute | solution.py:51
  271.7 7.2 %collective-permute-done.60 = bf16[128,1024]{1,0:T(8,128)(2,1)S(1)} collective-permute-done((bf16[128,1024]{1,0:T(8,128)(2,1)S(1)}, bf16[128,1024]{1,0:T(8,128)(2,1)S(1)}, u32[]{:S(2)}, u32[]{:S(2)}) %collective-permute-start.60) | collective-permute-done | bytes 262176 | tf_op jit(solution)/shard_map/ppermute | solution.py:51
  288.4 4.6 %all-to-all-start.6 = ((bf16[8,48,384]{2,1,0:T(8,128)(2,1)}), bf16[8,48,384]{2,1,0:T(8,128)(2,1)S(1)}, u32[]{:S(2)}, u32[]{:S(2)}) async-start(bf16[8,48,384]{2,1,0:T(8,128)(2,1)} %payload.1), calls=%async_computation.6 | async-start | bytes 589824 | tf_op jit(solution)/shard_map/all_to_all | solution.py:1461
  (323 shorter events, 159.4 us)
Async XLA Ops:
  22.1 26.9 %all-to-all-start = ((bf16[16,112,128]{2,1,0:T(8,128)(2,1)}), bf16[16,112,128]{2,1,0:T(8,128)(2,1)S(1)}, u32[]{:S(2)}, u32[]{:S(2)}) async-start(bf16[16,112,128]{2,1,0:T(8,128)(2,1)} %get-tuple-element.248), calls=%async_computation | async-start | bytes 917504 | tf_op jit(solution)/shard_map/all_to_all | solution.py:1168
  27.8 19.2 %collective-permute-start.7 = (bf16[2,64,1024]{2,1,0:T(8,128)(2,1)S(1)}, bf16[2,64,1024]{2,1,0:T(8,128)(2,1)S(1)}, u32[]{:S(2)}, u32[]{:S(2)}) collective-permute-start(bf16[2,64,1024]{2,1,0:T(8,128)(2,1)S(1)} %pad_maximum_fusion.refs_1_), channel_id=1, source_target_pairs={{0,22},{2,20},{4,18},{6,16},{16,6},{18,4},{20,2},{22,0},{1,23},{3,... | collective-permute-start | bytes 786440 | tf_op jit(solution)/shard_map/ppermute | solution.py:1167
  31.5 17.4 %collective-permute-start.4 = (bf16[2,64,1024]{2,1,0:T(8,128)(2,1)S(1)}, bf16[2,64,1024]{2,1,0:T(8,128)(2,1)S(1)}, u32[]{:S(2)}, u32[]{:S(2)}) collective-permute-start(bf16[2,64,1024]{2,1,0:T(8,128)(2,1)S(1)} %collective-permute-done.1.refs_5_), channel_id=1, source_target_pairs={{0,4},{4,0},{1,5},{5,1},{2,6},{6,2},{3,7},{7,3},{8,12},{12,8},{9,1... | collective-permute-start | bytes 786440 | tf_op jit(solution)/shard_map/ppermute | solution.py:51
  32.1 16.8 %collective-permute-start.5 = (bf16[2,64,1024]{2,1,0:T(8,128)(2,1)S(1)}, bf16[2,64,1024]{2,1,0:T(8,128)(2,1)S(1)}, u32[]{:S(2)}, u32[]{:S(2)}) collective-permute-start(bf16[2,64,1024]{2,1,0:T(8,128)(2,1)S(1)} %collective-permute-done.3.refs_2_), channel_id=1, source_target_pairs={{0,16},{16,0},{1,17},{17,1},{2,18},{18,2},{3,19},{19,3},{4,20},{20... | collective-permute-start | bytes 786440 | tf_op jit(solution)/shard_map/ppermute | solution.py:51
  32.7 16.3 %collective-permute-start.6 = (bf16[2,64,1024]{2,1,0:T(8,128)(2,1)S(1)}, bf16[2,64,1024]{2,1,0:T(8,128)(2,1)S(1)}, u32[]{:S(2)}, u32[]{:S(2)}) collective-permute-start(bf16[2,64,1024]{2,1,0:T(8,128)(2,1)S(1)} %collective-permute-done.2.refs_3_), channel_id=1, source_target_pairs={{0,2},{2,0},{1,3},{3,1},{4,6},{6,4},{5,7},{7,5},{8,10},{10,8},{9,1... | collective-permute-start | bytes 786440 | tf_op jit(solution)/shard_map/ppermute | solution.py:51
  50.8 16.6 %collective-permute-start.11 = (bf16[128,1024]{1,0:T(8,128)(2,1)}, bf16[128,1024]{1,0:T(8,128)(2,1)}, u32[]{:S(2)}, u32[]{:S(2)}) collective-permute-start(bf16[128,1024]{1,0:T(8,128)(2,1)} %refs_25_), channel_id=1, source_target_pairs={{0,8},{8,0},{1,9},{9,1},{2,10},{10,2},{3,11},{11,3},{4,12},{12,4},... | collective-permute-start | bytes 786440 | tf_op jit(solution)/shard_map/ppermute | solution.py:51
  52.5 15.0 %collective-permute-start.12 = (bf16[128,1024]{1,0:T(8,128)(2,1)}, bf16[128,1024]{1,0:T(8,128)(2,1)}, u32[]{:S(2)}, u32[]{:S(2)}) collective-permute-start(bf16[128,1024]{1,0:T(8,128)(2,1)} %refs_25_), channel_id=1, source_target_pairs={{0,4},{4,0},{1,5},{5,1},{2,6},{6,2},{3,7},{7,3},{8,12},{12,8},{9,1... | collective-permute-start | bytes 786440 | tf_op jit(solution)/shard_map/ppermute | solution.py:51
  71.9 14.3 %collective-permute-start.16 = (bf16[8,32,512]{2,1,0:T(8,128)(2,1)S(1)}, bf16[8,32,512]{2,1,0:T(8,128)(2,1)S(1)}, u32[]{:S(2)}, u32[]{:S(2)}) collective-permute-start(bf16[8,32,512]{2,1,0:T(8,128)(2,1)S(1)} %all-to-all-done.1), channel_id=1, source_target_pairs={{0,8},{8,0},{1,9},{9,1},{2,10},{10,2},{3,11},{11,3},{4,12},{12,4},... | collective-permute-start | bytes 786440 | tf_op jit(solution)/shard_map/ppermute | solution.py:51
  73.5 16.6 %collective-permute-start.17 = (bf16[8,32,512]{2,1,0:T(8,128)(2,1)S(1)}, bf16[8,32,512]{2,1,0:T(8,128)(2,1)S(1)}, u32[]{:S(2)}, u32[]{:S(2)}) collective-permute-start(bf16[8,32,512]{2,1,0:T(8,128)(2,1)S(1)} %all-to-all-done.1), channel_id=1, source_target_pairs={{0,4},{4,0},{1,5},{5,1},{2,6},{6,2},{3,7},{7,3},{8,12},{12,8},{9,1... | collective-permute-start | bytes 786440 | tf_op jit(solution)/shard_map/ppermute | solution.py:51
  75.5 21.4 %collective-permute-start.22 = (bf16[128,1024]{1,0:T(8,128)(2,1)}, bf16[128,1024]{1,0:T(8,128)(2,1)}, u32[]{:S(2)}, u32[]{:S(2)}) collective-permute-start(bf16[128,1024]{1,0:T(8,128)(2,1)} %collective-permute-done.11.refs_27_), channel_id=1, source_target_pairs={{0,4},{4,0},{1,5},{5,1},{2,6},{6,2},{3,7},{7,3},{8,12},{12,8},{9,1... | collective-permute-start | bytes 786440 | tf_op jit(solution)/shard_map/ppermute | solution.py:51
  83.8 15.1 %collective-permute-start.24 = (bf16[4,32,1024]{2,1,0:T(8,128)(2,1)S(1)}, bf16[4,32,1024]{2,1,0:T(8,128)(2,1)S(1)}, u32[]{:S(2)}, u32[]{:S(2)}) collective-permute-start(bf16[4,32,1024]{2,1,0:T(8,128)(2,1)S(1)} %pad_maximum_fusion.1.refs_4_.refs_6_), channel_id=1, source_target_pairs={{0,1},{1,0},{2,3},{3,2},{4,5},{5,4},{6,7},{7,6},{8,9},{9,8},{10,11... | collective-permute-start | bytes 786440 | tf_op jit(solution)/shard_map/ppermute | solution.py:51
  92.1 17.2 %all-to-all-start.2 = ((bf16[16,64,128]{2,1,0:T(8,128)(2,1)}), bf16[16,64,128]{2,1,0:T(8,128)(2,1)S(1)}, u32[]{:S(2)}, u32[]{:S(2)}) async-start(bf16[16,64,128]{2,1,0:T(8,128)(2,1)} %get-tuple-element.276), calls=%async_computation.2 | async-start | bytes 524288 | tf_op jit(solution)/shard_map/all_to_all | solution.py:1215
  159.3 18.3 %all-to-all-start.3 = ((bf16[4,128,1024]{2,1,0:T(8,128)(2,1)}), bf16[4,128,1024]{2,1,0:T(8,128)(2,1)S(1)}, u32[]{:S(2)}, u32[]{:S(2)}) async-start(bf16[4,128,1024]{2,1,0:T(8,128)(2,1)} %fold.1), calls=%async_computation.3 | async-start | bytes 2097152 | tf_op jit(solution)/shard_map/all_to_all | solution.py:1314
  163.2 14.4 %collective-permute-start.45 = (bf16[256,512]{1,0:T(8,128)(2,1)S(1)}, bf16[256,512]{1,0:T(8,128)(2,1)}, u32[]{:S(2)}, u32[]{:S(2)}) collective-permute-start(bf16[256,512]{1,0:T(8,128)(2,1)S(1)} %copy-done.72), channel_id=1, source_target_pairs={{0,8},{8,0},{1,9},{9,1},{2,10},{10,2},{3,11},{11,3},{4,12},{12,4},... | collective-permute-start | bytes 786440 | tf_op jit(solution)/shard_map/ppermute | solution.py:51
  184.0 15.9 %collective-permute-start.47 = (bf16[128,1024]{1,0:T(8,128)(2,1)}, bf16[128,1024]{1,0:T(8,128)(2,1)}, u32[]{:S(2)}, u32[]{:S(2)}) collective-permute-start(bf16[128,1024]{1,0:T(8,128)(2,1)} %get-tuple-element.344), channel_id=1, source_target_pairs={{0,4},{4,0},{1,5},{5,1},{2,6},{6,2},{3,7},{7,3},{8,12},{12,8},{9,1... | collective-permute-start | bytes 786440 | tf_op jit(solution)/shard_map/ppermute | solution.py:51
  185.6 16.7 %collective-permute-start.48 = (bf16[128,1024]{1,0:T(8,128)(2,1)}, bf16[128,1024]{1,0:T(8,128)(2,1)}, u32[]{:S(2)}, u32[]{:S(2)}) collective-permute-start(bf16[128,1024]{1,0:T(8,128)(2,1)} %get-tuple-element.345), channel_id=1, source_target_pairs={{0,8},{8,0},{1,9},{9,1},{2,10},{10,2},{3,11},{11,3},{4,12},{12,4},... | collective-permute-start | bytes 786440 | tf_op jit(solution)/shard_map/ppermute | solution.py:51
  188.2 18.6 %all-to-all-start.4 = ((bf16[16,64,128]{2,1,0:T(8,128)(2,1)}), bf16[16,64,128]{2,1,0:T(8,128)(2,1)S(1)}, u32[]{:S(2)}, u32[]{:S(2)}) async-start(bf16[16,64,128]{2,1,0:T(8,128)(2,1)} %get-tuple-element.343), calls=%async_computation.4 | async-start | bytes 524288 | tf_op jit(solution)/shard_map/all_to_all | solution.py:1354
  206.9 14.4 %collective-permute-start.51 = (bf16[512,1024]{1,0:T(8,128)(2,1)}, bf16[512,1024]{1,0:T(8,128)(2,1)S(1)}, u32[]{:S(2)}, u32[]{:S(2)}) collective-permute-start(bf16[512,1024]{1,0:T(8,128)(2,1)} %get-tuple-element.362), channel_id=1, source_target_pairs={{0,1},{1,0},{2,3},{3,2},{4,5},{5,4},{6,7},{7,6},{8,9},{9,8},{10,11... | collective-permute-start | bytes 3145736 | tf_op jit(solution)/shard_map/ppermute | solution.py:51
  206.9 14.4 %collective-permute-start.52 = (bf16[256,512]{1,0:T(8,128)(2,1)}, bf16[256,512]{1,0:T(8,128)(2,1)S(1)}, u32[]{:S(2)}, u32[]{:S(2)}) collective-permute-start(bf16[256,512]{1,0:T(8,128)(2,1)} %get-tuple-element.363), channel_id=1, source_target_pairs={{0,12},{4,8},{8,4},{12,0},{1,13},{5,9},{9,5},{13,1},{2,14},{6,10},... | collective-permute-start | bytes 786440 | tf_op jit(solution)/shard_map/ppermute | solution.py:1380
  239.6 43.4 %all-to-all-start.5 = ((bf16[8,2,64,1024]{3,2,1,0:T(8,128)(2,1)}), bf16[8,2,64,1024]{3,2,1,0:T(8,128)(2,1)}, u32[]{:S(2)}, u32[]{:S(2)}) async-start(bf16[8,2,64,1024]{3,2,1,0:T(8,128)(2,1)} %get-tuple-element.378), calls=%async_computation.5 | async-start | bytes 4194304 | tf_op jit(solution)/shard_map/all_to_all | solution.py:1405
  255.1 23.8 %collective-permute-start.57 = (bf16[2,192,384]{2,1,0:T(8,128)(2,1)S(1)}, bf16[2,192,384]{2,1,0:T(8,128)(2,1)S(1)}, u32[]{:S(2)}, u32[]{:S(2)}) collective-permute-start(bf16[2,192,384]{2,1,0:T(8,128)(2,1)S(1)} %get-tuple-element.401), channel_id=1, source_target_pairs={{0,8},{8,0},{1,9},{9,1},{2,10},{10,2},{3,11},{11,3},{4,12},{12,4},... | collective-permute-start | bytes 884744 | tf_op jit(solution)/shard_map/ppermute | solution.py:51
  257.4 14.3 %collective-permute-start.58 = (bf16[4,32,1024]{2,1,0:T(8,128)(2,1)S(1)}, bf16[4,32,1024]{2,1,0:T(8,128)(2,1)S(1)}, u32[]{:S(2)}, u32[]{:S(2)}) collective-permute-start(bf16[4,32,1024]{2,1,0:T(8,128)(2,1)S(1)} %get-tuple-element.403), channel_id=1, source_target_pairs={{0,2},{2,0},{1,3},{3,1},{4,6},{6,4},{5,7},{7,5},{8,10},{10,8},{9,1... | collective-permute-start | bytes 786440 | tf_op jit(solution)/shard_map/ppermute | solution.py:51
  259.0 19.9 %collective-permute-start.60 = (bf16[128,1024]{1,0:T(8,128)(2,1)S(1)}, bf16[128,1024]{1,0:T(8,128)(2,1)S(1)}, u32[]{:S(2)}, u32[]{:S(2)}) collective-permute-start(bf16[128,1024]{1,0:T(8,128)(2,1)S(1)} %pad_maximum_fusion.2), channel_id=1, source_target_pairs={{0,16},{16,0},{1,17},{17,1},{2,18},{18,2},{3,19},{19,3},{4,20},{20... | collective-permute-start | bytes 786440 | tf_op jit(solution)/shard_map/ppermute | solution.py:51
  288.4 17.0 %all-to-all-start.6 = ((bf16[8,48,384]{2,1,0:T(8,128)(2,1)}), bf16[8,48,384]{2,1,0:T(8,128)(2,1)S(1)}, u32[]{:S(2)}, u32[]{:S(2)}) async-start(bf16[8,48,384]{2,1,0:T(8,128)(2,1)} %payload.1), calls=%async_computation.6 | async-start | bytes 589824 | tf_op jit(solution)/shard_map/all_to_all | solution.py:1461
  (124 other events, 1156.6 us)
where the time goes:
time: 313 us; the launch traced here: 311 us
  starting transfers between devices  98.9 us (32%)
  waiting for transfers between devices  92.5 us (30%)
  Pallas kernels  90.3 us (29%)
  other arithmetic  14.4 us (5%)
  local copies, waits for them, and re-layouts  13.5 us (4%)
    pallas_call x17, Pallas kernels, call(): pl.pallas_call(body, in_specs=specs, out_specs=[hbm] * count_out, out_sha...  90.3 us
    ppermute x64, waiting for transfers between devices, swap(): return lax.ppermute(v, axis, [(0, 1), (1, 0)])  74.3 us
    ppermute x64, starting transfers between devices, swap(): return lax.ppermute(v, axis, [(0, 1), (1, 0)])  60.6 us
    ppermute x1, waiting for transfers between devices, fine_layer(): lax.ppermute(block, cube, [(i, 7 - i) for i in range(8)])  11.4 us
    unnamed x148, local copies, waits for them, and re-layouts  8.59 us
  transfers between devices with their start and end apart: 74, of which 31 were waited for; matrix products, arithmetic and copies ran while one was open for 5% of the time, Pallas kernels for 23%

commit v1 on v0

--- a/solution.py
+++ b/solution.py
@@ -686,6 +686,14 @@
     return k_pos <= q_pos
 
 
+def causal_t(q_share, k_share):
+    rows = lax.broadcasted_iota(jnp.int32, (TILE, TILE), 0)
+    cols = lax.broadcasted_iota(jnp.int32, (TILE, TILE), 1)
+    k_pos = (lax.shift_right_logical(rows, 6) * 2 + k_share) * 64 + (rows & 63)
+    q_pos = (lax.shift_right_logical(cols, 6) * 2 + q_share) * 64 + (cols & 63)
+    return k_pos <= q_pos
+
+
 def fine_forward_kernel(at, query, own, other, out, out_f, lse, s_ref):
     tiles = query.shape[0] // TILE
     c = at[4]
@@ -708,27 +716,14 @@
         for u in range(t + 1):
             top = score(u, top, u == t)
 
-        def expo(u, total):
+        total = jnp.zeros((TILE, 1), F32)
+        acc = jnp.zeros((TILE, HD), F32)
+        for u in range(t + 1):
             for n in range(2):
                 p = jnp.exp(s_ref[u * 2 + n] - top)
-                s_ref[u * 2 + n] = p
                 total = total + jnp.sum(p, -1, keepdims=True)
-            return total
-
-        total = jnp.zeros((TILE, 1), F32)
-        for u in range(t + 1):
-            total = expo(u, total)
-        inverse = 1.0 / total
-
-        def weigh(u, acc):
-            for n in range(2):
-                p = (s_ref[u * 2 + n] * inverse).astype(BF)
-                acc = acc + mm(p, both[n][aligned(u, TILE), pl.ds(HD, HD)])
-            return acc
-
-        acc = jnp.zeros((TILE, HD), F32)
-        for u in range(t + 1):
-            acc = weigh(u, acc)
+                acc = acc + mm(p.astype(BF), both[n][aligned(u, TILE), pl.ds(HD, HD)])
+        acc = acc * (1.0 / total)
         out_f[rows, :] = acc
         out[pl.ds(t * (TILE // 64), TILE // 64)] = acc.astype(BF).reshape(TILE // 64, 64, HD)
         lse[rows, :] = jnp.broadcast_to(top + jnp.log(total), (TILE, HD))
@@ -942,36 +937,30 @@
     keep[...] = jnp.zeros(keep.shape, keep.dtype)
     acc[...] = jnp.zeros_like(acc)
     totals = (keep, acc)
-
-    def tile(t, carry):
-        rows = aligned(t, TILE)
+    key_t = {}
+    for t in range(tiles):
+        rows = pl.ds(t * TILE, TILE)
         q = query[rows, :]
         go = go_ref[pl.ds(t * (TILE // 64), TILE // 64)].reshape(TILE, HD)
+        lse = jnp.transpose(lse_ref[rows, :])[0:1, :]
         delta = jnp.sum(go.astype(F32) * out_f[rows, :], -1, keepdims=True)
-        lse = lse_ref[rows, 0:1]
-
-        def one(u, gq, masked):
-            cols = aligned(u, TILE)
+        delta = jnp.transpose(jnp.broadcast_to(delta, (TILE, HD)))[0:1, :]
+        gq = jnp.zeros((HD, TILE), F32)
+        for u in range(t + 1):
+            cols = pl.ds(u * TILE, TILE)
             for n in range(2):
-                kk = both[n][cols, pl.ds(0, HD)]
-                p = jnp.exp(mm_nt(q, kk) * SCALE - lse)
-                if masked:
-                    p = jnp.where(causal(c, c if n == 0 else 1 - c), p, 0.0)
-                totals[n][cols, pl.ds(HD, HD)] += mm_tn(p.astype(BF), go)
-                ds = (p * (mm_nt(go, both[n][cols, pl.ds(HD, HD)]) - delta)).astype(BF)
-                totals[n][cols, pl.ds(0, HD)] += mm_tn(ds, q)
-                gq = gq + mm(ds, kk)
-            return gq
-
-        gq = jnp.zeros((TILE, HD), F32)
-        for u in range(t + 1):
-            gq = one(u, gq, u == t)
-        gq_ref[rows, :] = (gq * SCALE).astype(BF)
+                kk, vv = both[n][cols, pl.ds(0, HD)], both[n][cols, pl.ds(HD, HD)]
+                if u == t:
+                    key_t[u, n] = jnp.transpose(kk.astype(F32)).astype(BF)
+                p = jnp.exp(mm_nt(kk, q) * SCALE - lse)
+                if u == t:
+                    p = jnp.where(causal_t(c, c if n == 0 else 1 - c), p, 0.0)
+                totals[n][cols, pl.ds(HD, HD)] += mm(p.astype(BF), go)
+                ds = (p * (mm_nt(vv, go) - delta)).astype(BF)
+                totals[n][cols, pl.ds(0, HD)] += mm(ds, q)
+                gq = gq + mm(key_t[u, n], ds)
+        gq_ref[rows, :] = (jnp.transpose(gq) * SCALE).astype(BF)
         gq_ref.push(rows)
-        return carry
-
-    for t in range(tiles):
-        tile(t, 0)
     send[:, :HD] = (acc[:, :HD] * SCALE).astype(BF)
     send[:, HD:] = acc[:, HD:].astype(BF)
     send.push()
@@ -1031,9 +1020,13 @@
     per = left.shape[1] // 32
     transposed_product(big, left, right)
     spare = keep.shape[2] - sums.shape[1]
-    for q in range(16):
+
+    def deal(q, carry):
         keep[q, pl.ds(0, per), :] = big[aligned(2 * q + c, per), :]
         send[q, pl.ds(0, per), :] = big[aligned(2 * q + 1 - c, per), :].astype(BF)
+        return carry
+
+    lax.fori_loop(0, 16, deal, 0)
     pad = jnp.zeros((16, spare), F32)
     for q in range(16):
         pair = jnp.concatenate([sums[2 * q : 2 * q + 2, :], pad[:2]], 1)
@@ -1047,10 +1040,14 @@
     c = at[4]
     per = left.shape[1] // 32
     transposed_product(big, left, right)
-    for q in range(16):
-        rows = pl.ds(q * per, per)
+
+    def deal(q, carry):
+        rows = aligned(q, per)
         keep[rows, :] = big[aligned(2 * q + c, per), :]
         send[rows, :] = big[aligned(2 * q + 1 - c, per), :].astype(BF)
+        return carry
+
+    lax.fori_loop(0, 16, deal, 0)
 
 
 def input_kernel(at, keep, got, tokens, grad_middle, gains, grad_tokens):

time: 313 us -> 314 us (level)
  starting transfers between devices: 98.9 us -> 104 us
    ppermute x64, starting transfers between devices: 60.6 us -> 64.4 us  [swap(): return lax.ppermute(v, axis, [(0, 1), (1, 0)])]
  transfers between devices with their start and end apart: 74 -> 74, of which waited for: 31 -> 32; matrix products, arithmetic and copies ran while one was open for 5% -> 5% of each run, Pallas kernels for 23% -> 22%
where the time goes in v1:
time: 314 us; the launch traced here: 312 us
  starting transfers between devices  104 us (33%)
  waiting for transfers between devices  90.8 us (29%)
  Pallas kernels  88.5 us (28%)
  other arithmetic  14.4 us (5%)
  local copies, waits for them, and re-layouts  13.4 us (4%)
    pallas_call x17, Pallas kernels, call(): pl.pallas_call(body, in_specs=specs, out_specs=[hbm] * count_out, out_sha...  88.5 us
    ppermute x64, waiting for transfers between devices, swap(): return lax.ppermute(v, axis, [(0, 1), (1, 0)])  72 us
    ppermute x64, starting transfers between devices, swap(): return lax.ppermute(v, axis, [(0, 1), (1, 0)])  64.4 us
    ppermute x1, waiting for transfers between devices, fine_layer(): lax.ppermute(block, cube, [(i, 7 - i) for i in range(8)])  11.4 us
    unnamed x148, local copies, waits for them, and re-layouts  8.55 us
  transfers between devices with their start and end apart: 74, of which 32 were waited for; matrix products, arithmetic and copies ran while one was open for 5% of the time, Pallas kernels for 22%

profile of v1, /device:TPU:0, one launch (start us, length us, event | category | flops | bytes accessed | tf_op | source)
XLA Modules:
  0.0 312.4 jit_solution(11899291489207192953)
XLA Ops:
  1.7 4.1 %collective-permute-start = (bf16[64,1024]{1,0:T(8,128)(2,1)S(1)}, bf16[64,1024]{1,0:T(8,128)(2,1)S(1)}, u32[]{:S(2)}, u32[]{:S(2)}) collective-permute-start(bf16[64,1024]{1,0:T(8,128)(2,1)S(1)} %get-tuple-element.491), channel_id=1, source_target_pairs={{0,8},{8,0},{1,9},{9,1},{2,10},{10,2},{3,11},{11,3},{4,12},{12,4},... | collective-permute-start | bytes 393224 | tf_op jit(solution)/shard_map/ppermute | solution.py:51
  7.9 4.2 %collective-permute-done = bf16[64,1024]{1,0:T(8,128)(2,1)S(1)} collective-permute-done((bf16[64,1024]{1,0:T(8,128)(2,1)S(1)}, bf16[64,1024]{1,0:T(8,128)(2,1)S(1)}, u32[]{:S(2)}, u32[]{:S(2)}) %collective-permute-start) | collective-permute-done | bytes 131104 | tf_op jit(solution)/shard_map/ppermute | solution.py:51
  22.1 5.7 %all-to-all-start = ((bf16[16,112,128]{2,1,0:T(8,128)(2,1)}), bf16[16,112,128]{2,1,0:T(8,128)(2,1)S(1)}, u32[]{:S(2)}, u32[]{:S(2)}) async-start(bf16[16,112,128]{2,1,0:T(8,128)(2,1)} %get-tuple-element.248), calls=%async_computation | async-start | bytes 917504 | tf_op jit(solution)/shard_map/all_to_all | solution.py:1165
  35.6 11.4 %collective-permute-done.7.refs_8_ = bf16[2,64,1024]{2,1,0:T(8,128)(2,1)S(1)} collective-permute-done((bf16[2,64,1024]{2,1,0:T(8,128)(2,1)S(1)}, bf16[2,64,1024]{2,1,0:T(8,128)(2,1)S(1)}, u32[]{:S(2)}, u32[]{:S(2)}) %collective-permute-start.7) | collective-permute-done | bytes 262176 | tf_op jit(solution)/shard_map/ppermute | solution.py:1164
  60.3 7.2 %qkv.1 = (bf16[1024,1024]{1,0:T(8,128)(2,1)}, bf16[1024,128]{1,0:T(8,128)(2,1)}, bf16[1024,256]{1,0:T(8,128)(2,1)}, f32[8,1024]{1,0:T(8,128)}, bf16[1024,384]{1,0:T(8,128)(2,1)}) custom-call(s32[5]{0:T(128)} %stack.57.refs_0_, bf16[2,64,1024]{2,1,0:T(8,128)(2,1)} %copy-done.1, bf16[2,64,1024]{2,1,0:T(8,128)(2,1)} %copy-done.10, ...), custom_call_target="tpu_custom_call" | custom-call | tf_op jit(solution)/shard_map/qkv/pallas_call | solution.py:603
  75.5 5.4 %attention_forward.1 = (bf16[16,64,128]{2,1,0:T(8,128)(2,1)}, f32[1024,128]{1,0:T(8,128)}, f32[1024,128]{1,0:T(8,128)}, bf16[1024,128]{1,0:T(8,128)(2,1)}, bf16[...) custom-call(s32[5]{0:T(128)} %stack.57.refs_0_, bf16[1024,128]{1,0:T(8,128)(2,1)} %get-tuple-element.265.refs_1_, ...), custom_call_target="tpu_custom_call" | custom-call | tf_op jit(solution)/shard_map/attention_forward/pallas_call | solution.py:603
  92.1 4.7 %all-to-all-start.2 = ((bf16[16,64,128]{2,1,0:T(8,128)(2,1)}), bf16[16,64,128]{2,1,0:T(8,128)(2,1)S(1)}, u32[]{:S(2)}, u32[]{:S(2)}) async-start(bf16[16,64,128]{2,1,0:T(8,128)(2,1)} %get-tuple-element.276), calls=%async_computation.2 | async-start | bytes 524288 | tf_op jit(solution)/shard_map/all_to_all | solution.py:1212
  100.6 7.3 %collective-permute-done.21.refs_7_.refs_9_ = bf16[4,32,1024]{2,1,0:T(8,128)(2,1)S(1)} collective-permute-done((bf16[4,32,1024]{2,1,0:T(8,128)(2,1)S(1)}, bf16[4,32,1024]{2,1,0:T(8,128)(2,1)S(1)}, u32[]{:S(2)}, u32[]{:S(2)}) %collective-permute-start.21) | collective-permute-done | bytes 262176 | tf_op jit(solution)/shard_map/ppermute | solution.py:51
  111.7 4.6 %middle.1 = (bf16[128,1024]{1,0:T(8,128)(2,1)}, f32[128,1024]{1,0:T(8,128)}, f32[128,1024]{1,0:T(8,128)}, f32[128,128]{1,0:T(8,128)}, bf16[128,1024]{1,0:T(8,128)(2,1)}) custom-call(s32[5]{0:T(128)} %stack.57.refs_0_, bf16[16,64,128]{2,1,0:T(8,128)(2,1)} %copy-done.23, bf16[2,64,1024]{2,1,0:T(8,128)(2,1)} %refs_3_.1, ...), custom_call_target="tpu_custom_call" | custom-call | tf_op jit(solution)/shard_map/middle/pallas_call | solution.py:603
  123.2 4.9 %collective-permute-done.28.refs_2_ = bf16[128,1024]{1,0:T(8,128)(2,1)S(1)} collective-permute-done((bf16[128,1024]{1,0:T(8,128)(2,1)}, bf16[128,1024]{1,0:T(8,128)(2,1)S(1)}, u32[]{:S(2)}, u32[]{:S(2)}) %collective-permute-start.28) | collective-permute-done | bytes 262176 | tf_op jit(solution)/shard_map/ppermute | solution.py:51
  139.3 9.3 %inner.1 = (bf16[1024,1024]{1,0:T(8,128)(2,1)}, bf16[1024,1024]{1,0:T(8,128)(2,1)}, bf16[512,1024]{1,0:T(8,128)(2,1)}, bf16[1024,512]{1,0:T(8,128)(2,1)}, bf16[1...) custom-call(s32[5]{0:T(128)} %stack.57.refs_0_, ...), custom_call_target="tpu_custom_call" | custom-call | tf_op jit(solution)/shard_map/inner/pallas_call | solution.py:603
  148.9 5.7 %inner_grad.1 = (f32[256,512]{1,0:T(8,128)}, bf16[256,512]{1,0:T(8,128)(2,1)}, bf16[256,512]{1,0:T(8,128)(2,1)}, bf16[256,512]{1,0:T(8,128)(2,1)}) custom-call(s32[5]{0:T(128)} %stack.57.refs_0_, bf16[1024,1024]{1,0:T(8,128)(2,1)} %get-tuple-element.315.refs_1_, bf16[1024,512]{1,0:T(8,128)(2,1)} %get-tuple-element.316.refs_2_), custom_call_target="tpu_custom_call" | custom-call | tf_op jit(solution)/shard_map/inner_grad/pallas_call | solution.py:603
  165.6 7.9 %outer_grad.1 = (f32[128,1024]{1,0:T(8,128)}, bf16[128,1024]{1,0:T(8,128)(2,1)}, bf16[128,1024]{1,0:T(8,128)(2,1)}, bf16[128,1024]{1,0:T(8,128)(2,1)}, f32[512,1024]{1,0:T(8,128)}, /*index=5*/bf16[512,1024]{1,0:T(8,128)(2,1)}) custom-call(s32[5]{0:T(128)} %stack.57.refs_0_, bf16[1024,512]{1,0:T(8,128)(2,1)} %get-tuple-element.325.refs_1_, ...), custom_call_target="tpu_custom_call" | custom-call | tf_op jit(solution)/shard_map/outer_grad/pallas_call | solution.py:603
  178.6 5.3 %branch.1 = (f32[128,1024]{1,0:T(8,128)}, bf16[128,1024]{1,0:T(8,128)(2,1)}, bf16[16,64,128]{2,1,0:T(8,128)(2,1)}, f32[2,1024]{1,0:T(2,128)}) custom-call(s32[5]{0:T(128)} %stack.57.refs_0_, bf16[4,128,1024]{2,1,0:T(8,128)(2,1)} %copy-done, f32[128,1024]{1,0:T(8,128)} %get-tuple-element.336.refs_2_, f32[128,128]{1,0:T(8,128)} %get-tuple-element.337.refs_3_, ...), custom_call_target="tpu_custom_call" | custom-call | tf_op jit(solution)/shard_map/branch/pallas_call | solution.py:603
  194.2 5.1 %out_grad.1 = (f32[512,1024]{1,0:T(8,128)}, bf16[512,1024]{1,0:T(8,128)(2,1)}) custom-call(s32[5]{0:T(128)} %stack.57.refs_0_, bf16[128,1024]{1,0:T(8,128)(2,1)} %get-tuple-element.348.refs_1_, bf16[128,1024]{1,0:T(8,128)(2,1)} %get-tuple-element.349.refs_2_), custom_call_target="tpu_custom_call" | custom-call | tf_op jit(solution)/shard_map/out_grad/pallas_call | solution.py:603
  202.3 4.6 %all-to-all-done.4.refs_4_ = bf16[16,64,128]{2,1,0:T(8,128)(2,1)S(1)} async-done(((bf16[16,64,128]{2,1,0:T(8,128)(2,1)}), bf16[16,64,128]{2,1,0:T(8,128)(2,1)S(1)}, u32[]{:S(2)}, u32[]{:S(2)}) %all-to-all-start.4) | async-done | bytes 262176 | tf_op jit(solution)/shard_map/all_to_all | solution.py:1351
  210.6 9.0 %attention_backward.1 = (bf16[1024,128]{1,0:T(8,128)(2,1)}, f32[1024,256]{1,0:T(8,128)}, bf16[1024,256]{1,0:T(8,128)(2,1)}) custom-call(s32[5]{0:T(128)} %stack.57.refs_0_, bf16[1024,128]{1,0:T(8,128)(2,1)} %get-tuple-element.270.refs_1_, bf16[1024,256]{1,0:T(8,128)(2,1)} %get-tuple-element.271.refs_2_, bf16[1024,256]{1,0:T(8,128)(2,1)} %get-tuple-element.272.refs_3_, ...), custom_call_target="tpu_custom_call" | custom-call | tf_op jit(solution)/shard_map/attention_backward/pallas_call | solution.py:603
  226.5 6.3 %partial.1 = (bf16[1024,384]{1,0:T(8,128)(2,1)}, bf16[8,2,64,1024]{3,2,1,0:T(8,128)(2,1)}, f32[2,1024]{1,0:T(2,128)}) custom-call(s32[5]{0:T(128)} %stack.57.refs_0_, bf16[2,64,1024]{2,1,0:T(8,128)(2,1)} %copy-done.1, bf16[2,64,1024]{2,1,0:T(8,128)(2,1)} %copy-done.10, bf16[2,64,1024]{2,1,0:T(8,128)(2,1)} %copy-done.9, bf16[2,64,1024]{2,1,0:T(8,128)(2,1)} %copy-done.14, ...), custom_call_target="tpu_custom_call" | custom-call | tf_op jit(solution)/shard_map/partial/pallas_call | solution.py:603
  238.1 5.0 %all-to-all-start.5 = ((bf16[8,2,64,1024]{3,2,1,0:T(8,128)(2,1)}), bf16[8,2,64,1024]{3,2,1,0:T(8,128)(2,1)}, u32[]{:S(2)}, u32[]{:S(2)}) async-start(bf16[8,2,64,1024]{3,2,1,0:T(8,128)(2,1)} %get-tuple-element.378), calls=%async_computation.5 | async-start | bytes 4194304 | tf_op jit(solution)/shard_map/all_to_all | solution.py:1402
  244.7 6.0 %head_grad.1 = (f32[16,48,384]{2,1,0:T(8,128)}, bf16[16,48,384]{2,1,0:T(8,128)(2,1)}) custom-call(s32[5]{0:T(128)} %stack.57.refs_0_, bf16[1024,1024]{1,0:T(8,128)(2,1)} %get-tuple-element.379.refs_1_, bf16[1024,384]{1,0:T(8,128)(2,1)} %get-tuple-element.380.refs_2_, f32[32,128]{1,0:T(8,128)} %reshape.313.refs_3_), custom_call_target="tpu_custom_call" | custom-call | tf_op jit(solution)/shard_map/head_grad/pallas_call | solution.py:603
  262.2 9.2 %collective-permute-done.58 = bf16[4,32,1024]{2,1,0:T(8,128)(2,1)S(1)} collective-permute-done((bf16[4,32,1024]{2,1,0:T(8,128)(2,1)S(1)}, bf16[4,32,1024]{2,1,0:T(8,128)(2,1)S(1)}, u32[]{:S(2)}, u32[]{:S(2)}) %collective-permute-start.58) | collective-permute-done | bytes 262176 | tf_op jit(solution)/shard_map/ppermute | solution.py:51
  271.4 4.0 %collective-permute-done.57.refs_1_ = bf16[2,192,384]{2,1,0:T(8,128)(2,1)S(1)} collective-permute-done((bf16[2,192,384]{2,1,0:T(8,128)(2,1)S(1)}, bf16[2,192,384]{2,1,0:T(8,128)(2,1)S(1)}, u32[]{:S(2)}, u32[]{:S(2)}) %collective-permute-start.57) | collective-permute-done | bytes 294944 | tf_op jit(solution)/shard_map/ppermute | solution.py:51
  282.8 5.9 %collective-permute-start.61 = (bf16[64,1024]{1,0:T(8,128)(2,1)}, bf16[64,1024]{1,0:T(8,128)(2,1)S(1)}, u32[]{:S(2)}, u32[]{:S(2)}) collective-permute-start(bf16[64,1024]{1,0:T(8,128)(2,1)} %get-tuple-element.426), channel_id=1, source_target_pairs={{0,8},{8,0},{1,9},{9,1},{2,10},{10,2},{3,11},{11,3},{4,12},{12,4},... | collective-permute-start | bytes 393224 | tf_op jit(solution)/shard_map/ppermute | solution.py:51
  288.7 5.1 %all-to-all-start.6 = ((bf16[8,48,384]{2,1,0:T(8,128)(2,1)}), bf16[8,48,384]{2,1,0:T(8,128)(2,1)S(1)}, u32[]{:S(2)}, u32[]{:S(2)}) async-start(bf16[8,48,384]{2,1,0:T(8,128)(2,1)} %payload.1), calls=%async_computation.6 | async-start | bytes 589824 | tf_op jit(solution)/shard_map/all_to_all | solution.py:1458
  (323 shorter events, 162.6 us)
Async XLA Ops:
  22.1 26.9 %all-to-all-start = ((bf16[16,112,128]{2,1,0:T(8,128)(2,1)}), bf16[16,112,128]{2,1,0:T(8,128)(2,1)S(1)}, u32[]{:S(2)}, u32[]{:S(2)}) async-start(bf16[16,112,128]{2,1,0:T(8,128)(2,1)} %get-tuple-element.248), calls=%async_computation | async-start | bytes 917504 | tf_op jit(solution)/shard_map/all_to_all | solution.py:1165
  27.8 19.2 %collective-permute-start.7 = (bf16[2,64,1024]{2,1,0:T(8,128)(2,1)S(1)}, bf16[2,64,1024]{2,1,0:T(8,128)(2,1)S(1)}, u32[]{:S(2)}, u32[]{:S(2)}) collective-permute-start(bf16[2,64,1024]{2,1,0:T(8,128)(2,1)S(1)} %pad_maximum_fusion.refs_1_), channel_id=1, source_target_pairs={{0,22},{2,20},{4,18},{6,16},{16,6},{18,4},{20,2},{22,0},{1,23},{3,... | collective-permute-start | bytes 786440 | tf_op jit(solution)/shard_map/ppermute | solution.py:1164
  31.5 17.4 %collective-permute-start.4 = (bf16[2,64,1024]{2,1,0:T(8,128)(2,1)S(1)}, bf16[2,64,1024]{2,1,0:T(8,128)(2,1)S(1)}, u32[]{:S(2)}, u32[]{:S(2)}) collective-permute-start(bf16[2,64,1024]{2,1,0:T(8,128)(2,1)S(1)} %collective-permute-done.1.refs_5_), channel_id=1, source_target_pairs={{0,4},{4,0},{1,5},{5,1},{2,6},{6,2},{3,7},{7,3},{8,12},{12,8},{9,1... | collective-permute-start | bytes 786440 | tf_op jit(solution)/shard_map/ppermute | solution.py:51
  32.1 16.8 %collective-permute-start.5 = (bf16[2,64,1024]{2,1,0:T(8,128)(2,1)S(1)}, bf16[2,64,1024]{2,1,0:T(8,128)(2,1)S(1)}, u32[]{:S(2)}, u32[]{:S(2)}) collective-permute-start(bf16[2,64,1024]{2,1,0:T(8,128)(2,1)S(1)} %collective-permute-done.3.refs_2_), channel_id=1, source_target_pairs={{0,16},{16,0},{1,17},{17,1},{2,18},{18,2},{3,19},{19,3},{4,20},{20... | collective-permute-start | bytes 786440 | tf_op jit(solution)/shard_map/ppermute | solution.py:51
  32.7 16.3 %collective-permute-start.6 = (bf16[2,64,1024]{2,1,0:T(8,128)(2,1)S(1)}, bf16[2,64,1024]{2,1,0:T(8,128)(2,1)S(1)}, u32[]{:S(2)}, u32[]{:S(2)}) collective-permute-start(bf16[2,64,1024]{2,1,0:T(8,128)(2,1)S(1)} %collective-permute-done.2.refs_3_), channel_id=1, source_target_pairs={{0,2},{2,0},{1,3},{3,1},{4,6},{6,4},{5,7},{7,5},{8,10},{10,8},{9,1... | collective-permute-start | bytes 786440 | tf_op jit(solution)/shard_map/ppermute | solution.py:51
  32.8 14.2 %collective-permute-start.8 = (bf16[32,1024]{1,0:T(8,128)(2,1)S(1)}, bf16[32,1024]{1,0:T(8,128)(2,1)S(1)}, u32[]{:S(2)}, u32[]{:S(2)}) collective-permute-start(bf16[32,1024]{1,0:T(8,128)(2,1)S(1)} %copy-done.54), channel_id=1, source_target_pairs={{0,8},{8,0},{1,9},{9,1},{2,10},{10,2},{3,11},{11,3},{4,12},{12,4},... | collective-permute-start | bytes 196616 | tf_op jit(solution)/shard_map/ppermute | solution.py:51
  50.8 16.6 %collective-permute-start.11 = (bf16[128,1024]{1,0:T(8,128)(2,1)}, bf16[128,1024]{1,0:T(8,128)(2,1)}, u32[]{:S(2)}, u32[]{:S(2)}) collective-permute-start(bf16[128,1024]{1,0:T(8,128)(2,1)} %refs_25_), channel_id=1, source_target_pairs={{0,8},{8,0},{1,9},{9,1},{2,10},{10,2},{3,11},{11,3},{4,12},{12,4},... | collective-permute-start | bytes 786440 | tf_op jit(solution)/shard_map/ppermute | solution.py:51
  52.5 15.0 %collective-permute-start.12 = (bf16[128,1024]{1,0:T(8,128)(2,1)}, bf16[128,1024]{1,0:T(8,128)(2,1)}, u32[]{:S(2)}, u32[]{:S(2)}) collective-permute-start(bf16[128,1024]{1,0:T(8,128)(2,1)} %refs_25_), channel_id=1, source_target_pairs={{0,4},{4,0},{1,5},{5,1},{2,6},{6,2},{3,7},{7,3},{8,12},{12,8},{9,1... | collective-permute-start | bytes 786440 | tf_op jit(solution)/shard_map/ppermute | solution.py:51
  69.7 14.1 %collective-permute-start.14 = (bf16[4,32,1024]{2,1,0:T(8,128)(2,1)S(1)}, bf16[4,32,1024]{2,1,0:T(8,128)(2,1)S(1)}, u32[]{:S(2)}, u32[]{:S(2)}) collective-permute-start(bf16[4,32,1024]{2,1,0:T(8,128)(2,1)S(1)} %pad_maximum_fusion.1.refs_4_.refs_6_), channel_id=1, source_target_pairs={{0,4},{4,0},{1,5},{5,1},{2,6},{6,2},{3,7},{7,3},{8,12},{12,8},{9,1... | collective-permute-start | bytes 786440 | tf_op jit(solution)/shard_map/ppermute | solution.py:51
  71.9 14.3 %collective-permute-start.16 = (bf16[8,32,512]{2,1,0:T(8,128)(2,1)S(1)}, bf16[8,32,512]{2,1,0:T(8,128)(2,1)S(1)}, u32[]{:S(2)}, u32[]{:S(2)}) collective-permute-start(bf16[8,32,512]{2,1,0:T(8,128)(2,1)S(1)} %all-to-all-done.1), channel_id=1, source_target_pairs={{0,8},{8,0},{1,9},{9,1},{2,10},{10,2},{3,11},{11,3},{4,12},{12,4},... | collective-permute-start | bytes 786440 | tf_op jit(solution)/shard_map/ppermute | solution.py:51
  73.5 16.6 %collective-permute-start.17 = (bf16[8,32,512]{2,1,0:T(8,128)(2,1)S(1)}, bf16[8,32,512]{2,1,0:T(8,128)(2,1)S(1)}, u32[]{:S(2)}, u32[]{:S(2)}) collective-permute-start(bf16[8,32,512]{2,1,0:T(8,128)(2,1)S(1)} %all-to-all-done.1), channel_id=1, source_target_pairs={{0,4},{4,0},{1,5},{5,1},{2,6},{6,2},{3,7},{7,3},{8,12},{12,8},{9,1... | collective-permute-start | bytes 786440 | tf_op jit(solution)/shard_map/ppermute | solution.py:51
  75.5 21.4 %collective-permute-start.22 = (bf16[128,1024]{1,0:T(8,128)(2,1)}, bf16[128,1024]{1,0:T(8,128)(2,1)}, u32[]{:S(2)}, u32[]{:S(2)}) collective-permute-start(bf16[128,1024]{1,0:T(8,128)(2,1)} %collective-permute-done.11.refs_27_), channel_id=1, source_target_pairs={{0,4},{4,0},{1,5},{5,1},{2,6},{6,2},{3,7},{7,3},{8,12},{12,8},{9,1... | collective-permute-start | bytes 786440 | tf_op jit(solution)/shard_map/ppermute | solution.py:51
  83.8 15.1 %collective-permute-start.24 = (bf16[4,32,1024]{2,1,0:T(8,128)(2,1)S(1)}, bf16[4,32,1024]{2,1,0:T(8,128)(2,1)S(1)}, u32[]{:S(2)}, u32[]{:S(2)}) collective-permute-start(bf16[4,32,1024]{2,1,0:T(8,128)(2,1)S(1)} %pad_maximum_fusion.1.refs_4_.refs_6_), channel_id=1, source_target_pairs={{0,1},{1,0},{2,3},{3,2},{4,5},{5,4},{6,7},{7,6},{8,9},{9,8},{10,11... | collective-permute-start | bytes 786440 | tf_op jit(solution)/shard_map/ppermute | solution.py:51
  92.1 17.2 %all-to-all-start.2 = ((bf16[16,64,128]{2,1,0:T(8,128)(2,1)}), bf16[16,64,128]{2,1,0:T(8,128)(2,1)S(1)}, u32[]{:S(2)}, u32[]{:S(2)}) async-start(bf16[16,64,128]{2,1,0:T(8,128)(2,1)} %get-tuple-element.276), calls=%async_computation.2 | async-start | bytes 524288 | tf_op jit(solution)/shard_map/all_to_all | solution.py:1212
  159.3 18.3 %all-to-all-start.3 = ((bf16[4,128,1024]{2,1,0:T(8,128)(2,1)}), bf16[4,128,1024]{2,1,0:T(8,128)(2,1)S(1)}, u32[]{:S(2)}, u32[]{:S(2)}) async-start(bf16[4,128,1024]{2,1,0:T(8,128)(2,1)} %fold.1), calls=%async_computation.3 | async-start | bytes 2097152 | tf_op jit(solution)/shard_map/all_to_all | solution.py:1311
  162.9 14.1 %collective-permute-start.44 = (bf16[256,512]{1,0:T(8,128)(2,1)S(1)}, bf16[256,512]{1,0:T(8,128)(2,1)S(1)}, u32[]{:S(2)}, u32[]{:S(2)}) collective-permute-start(bf16[256,512]{1,0:T(8,128)(2,1)S(1)} %copy-done.73), channel_id=1, source_target_pairs={{0,4},{4,0},{1,5},{5,1},{2,6},{6,2},{3,7},{7,3},{8,12},{12,8},{9,1... | collective-permute-start | bytes 786440 | tf_op jit(solution)/shard_map/ppermute | solution.py:51
  163.2 14.4 %collective-permute-start.45 = (bf16[256,512]{1,0:T(8,128)(2,1)S(1)}, bf16[256,512]{1,0:T(8,128)(2,1)}, u32[]{:S(2)}, u32[]{:S(2)}) collective-permute-start(bf16[256,512]{1,0:T(8,128)(2,1)S(1)} %copy-done.72), channel_id=1, source_target_pairs={{0,8},{8,0},{1,9},{9,1},{2,10},{10,2},{3,11},{11,3},{4,12},{12,4},... | collective-permute-start | bytes 786440 | tf_op jit(solution)/shard_map/ppermute | solution.py:51
  184.0 16.1 %collective-permute-start.47 = (bf16[128,1024]{1,0:T(8,128)(2,1)}, bf16[128,1024]{1,0:T(8,128)(2,1)}, u32[]{:S(2)}, u32[]{:S(2)}) collective-permute-start(bf16[128,1024]{1,0:T(8,128)(2,1)} %get-tuple-element.344), channel_id=1, source_target_pairs={{0,4},{4,0},{1,5},{5,1},{2,6},{6,2},{3,7},{7,3},{8,12},{12,8},{9,1... | collective-permute-start | bytes 786440 | tf_op jit(solution)/shard_map/ppermute | solution.py:51
  185.6 16.7 %collective-permute-start.48 = (bf16[128,1024]{1,0:T(8,128)(2,1)}, bf16[128,1024]{1,0:T(8,128)(2,1)}, u32[]{:S(2)}, u32[]{:S(2)}) collective-permute-start(bf16[128,1024]{1,0:T(8,128)(2,1)} %get-tuple-element.345), channel_id=1, source_target_pairs={{0,8},{8,0},{1,9},{9,1},{2,10},{10,2},{3,11},{11,3},{4,12},{12,4},... | collective-permute-start | bytes 786440 | tf_op jit(solution)/shard_map/ppermute | solution.py:51
  188.2 18.6 %all-to-all-start.4 = ((bf16[16,64,128]{2,1,0:T(8,128)(2,1)}), bf16[16,64,128]{2,1,0:T(8,128)(2,1)S(1)}, u32[]{:S(2)}, u32[]{:S(2)}) async-start(bf16[16,64,128]{2,1,0:T(8,128)(2,1)} %get-tuple-element.343), calls=%async_computation.4 | async-start | bytes 524288 | tf_op jit(solution)/shard_map/all_to_all | solution.py:1351
  238.1 42.0 %all-to-all-start.5 = ((bf16[8,2,64,1024]{3,2,1,0:T(8,128)(2,1)}), bf16[8,2,64,1024]{3,2,1,0:T(8,128)(2,1)}, u32[]{:S(2)}, u32[]{:S(2)}) async-start(bf16[8,2,64,1024]{3,2,1,0:T(8,128)(2,1)} %get-tuple-element.378), calls=%async_computation.5 | async-start | bytes 4194304 | tf_op jit(solution)/shard_map/all_to_all | solution.py:1402
  254.0 21.4 %collective-permute-start.57 = (bf16[2,192,384]{2,1,0:T(8,128)(2,1)S(1)}, bf16[2,192,384]{2,1,0:T(8,128)(2,1)S(1)}, u32[]{:S(2)}, u32[]{:S(2)}) collective-permute-start(bf16[2,192,384]{2,1,0:T(8,128)(2,1)S(1)} %get-tuple-element.401), channel_id=1, source_target_pairs={{0,8},{8,0},{1,9},{9,1},{2,10},{10,2},{3,11},{11,3},{4,12},{12,4},... | collective-permute-start | bytes 884744 | tf_op jit(solution)/shard_map/ppermute | solution.py:51
  256.8 14.6 %collective-permute-start.58 = (bf16[4,32,1024]{2,1,0:T(8,128)(2,1)S(1)}, bf16[4,32,1024]{2,1,0:T(8,128)(2,1)S(1)}, u32[]{:S(2)}, u32[]{:S(2)}) collective-permute-start(bf16[4,32,1024]{2,1,0:T(8,128)(2,1)S(1)} %get-tuple-element.403), channel_id=1, source_target_pairs={{0,2},{2,0},{1,3},{3,1},{4,6},{6,4},{5,7},{7,5},{8,10},{10,8},{9,1... | collective-permute-start | bytes 786440 | tf_op jit(solution)/shard_map/ppermute | solution.py:51
  288.7 17.7 %all-to-all-start.6 = ((bf16[8,48,384]{2,1,0:T(8,128)(2,1)}), bf16[8,48,384]{2,1,0:T(8,128)(2,1)S(1)}, u32[]{:S(2)}, u32[]{:S(2)}) async-start(bf16[8,48,384]{2,1,0:T(8,128)(2,1)} %payload.1), calls=%async_computation.6 | async-start | bytes 589824 | tf_op jit(solution)/shard_map/all_to_all | solution.py:1458
  (124 other events, 1167.4 us)

commit v2 on v0

--- a/solution.py
+++ b/solution.py
@@ -708,27 +708,14 @@
         for u in range(t + 1):
             top = score(u, top, u == t)
 
-        def expo(u, total):
+        total = jnp.zeros((TILE, 1), F32)
+        acc = jnp.zeros((TILE, HD), F32)
+        for u in range(t + 1):
             for n in range(2):
                 p = jnp.exp(s_ref[u * 2 + n] - top)
-                s_ref[u * 2 + n] = p
                 total = total + jnp.sum(p, -1, keepdims=True)
-            return total
-
-        total = jnp.zeros((TILE, 1), F32)
-        for u in range(t + 1):
-            total = expo(u, total)
-        inverse = 1.0 / total
-
-        def weigh(u, acc):
-            for n in range(2):
-                p = (s_ref[u * 2 + n] * inverse).astype(BF)
-                acc = acc + mm(p, both[n][aligned(u, TILE), pl.ds(HD, HD)])
-            return acc
-
-        acc = jnp.zeros((TILE, HD), F32)
-        for u in range(t + 1):
-            acc = weigh(u, acc)
+                acc = acc + mm(p.astype(BF), both[n][aligned(u, TILE), pl.ds(HD, HD)])
+        acc = acc * (1.0 / total)
         out_f[rows, :] = acc
         out[pl.ds(t * (TILE // 64), TILE // 64)] = acc.astype(BF).reshape(TILE // 64, 64, HD)
         lse[rows, :] = jnp.broadcast_to(top + jnp.log(total), (TILE, HD))
@@ -1047,10 +1034,14 @@
     c = at[4]
     per = left.shape[1] // 32
     transposed_product(big, left, right)
-    for q in range(16):
-        rows = pl.ds(q * per, per)
+
+    def deal(q, carry):
+        rows = aligned(q, per)
         keep[rows, :] = big[aligned(2 * q + c, per), :]
         send[rows, :] = big[aligned(2 * q + 1 - c, per), :].astype(BF)
+        return carry
+
+    lax.fori_loop(0, 16, deal, 0)
 
 
 def input_kernel(at, keep, got, tokens, grad_middle, gains, grad_tokens):

time: 313 us -> 313 us (level)
  transfers between devices with their start and end apart: 74 -> 74, of which waited for: 31 -> 31; matrix products, arithmetic and copies ran while one was open for 5% -> 5% of each run, Pallas kernels for 23% -> 22%
where the time goes in v2:
time: 313 us; the launch traced here: 311 us
  starting transfers between devices  98.9 us (32%)
  waiting for transfers between devices  92.9 us (30%)
  Pallas kernels  89.9 us (29%)
  other arithmetic  14.4 us (5%)
  local copies, waits for them, and re-layouts  13.5 us (4%)
    pallas_call x17, Pallas kernels, call(): pl.pallas_call(body, in_specs=specs, out_specs=[hbm] * count_out, out_sha...  89.9 us
    ppermute x64, waiting for transfers between devices, swap(): return lax.ppermute(v, axis, [(0, 1), (1, 0)])  74.7 us
    ppermute x64, starting transfers between devices, swap(): return lax.ppermute(v, axis, [(0, 1), (1, 0)])  60.6 us
    ppermute x1, waiting for transfers between devices, fine_layer(): lax.ppermute(block, cube, [(i, 7 - i) for i in range(8)])  11.4 us
    unnamed x148, local copies, waits for them, and re-layouts  8.59 us
  transfers between devices with their start and end apart: 74, of which 31 were waited for; matrix products, arithmetic and copies ran while one was open for 5% of the time, Pallas kernels for 22%

profile of v2, /device:TPU:0, one launch (start us, length us, event | category | flops | bytes accessed | tf_op | source)
XLA Modules:
  0.0 311.4 jit_solution(2472122129991345212)
XLA Ops:
  1.7 4.1 %collective-permute-start = (bf16[64,1024]{1,0:T(8,128)(2,1)S(1)}, bf16[64,1024]{1,0:T(8,128)(2,1)S(1)}, u32[]{:S(2)}, u32[]{:S(2)}) collective-permute-start(bf16[64,1024]{1,0:T(8,128)(2,1)S(1)} %get-tuple-element.491), channel_id=1, source_target_pairs={{0,8},{8,0},{1,9},{9,1},{2,10},{10,2},{3,11},{11,3},{4,12},{12,4},... | collective-permute-start | bytes 393224 | tf_op jit(solution)/shard_map/ppermute | solution.py:51
  7.9 4.2 %collective-permute-done = bf16[64,1024]{1,0:T(8,128)(2,1)S(1)} collective-permute-done((bf16[64,1024]{1,0:T(8,128)(2,1)S(1)}, bf16[64,1024]{1,0:T(8,128)(2,1)S(1)}, u32[]{:S(2)}, u32[]{:S(2)}) %collective-permute-start) | collective-permute-done | bytes 131104 | tf_op jit(solution)/shard_map/ppermute | solution.py:51
  22.1 5.7 %all-to-all-start = ((bf16[16,112,128]{2,1,0:T(8,128)(2,1)}), bf16[16,112,128]{2,1,0:T(8,128)(2,1)S(1)}, u32[]{:S(2)}, u32[]{:S(2)}) async-start(bf16[16,112,128]{2,1,0:T(8,128)(2,1)} %get-tuple-element.248), calls=%async_computation | async-start | bytes 917504 | tf_op jit(solution)/shard_map/all_to_all | solution.py:1159
  35.6 11.4 %collective-permute-done.7.refs_8_ = bf16[2,64,1024]{2,1,0:T(8,128)(2,1)S(1)} collective-permute-done((bf16[2,64,1024]{2,1,0:T(8,128)(2,1)S(1)}, bf16[2,64,1024]{2,1,0:T(8,128)(2,1)S(1)}, u32[]{:S(2)}, u32[]{:S(2)}) %collective-permute-start.7) | collective-permute-done | bytes 262176 | tf_op jit(solution)/shard_map/ppermute | solution.py:1158
  60.3 7.2 %qkv.1 = (bf16[1024,1024]{1,0:T(8,128)(2,1)}, bf16[1024,128]{1,0:T(8,128)(2,1)}, bf16[1024,256]{1,0:T(8,128)(2,1)}, f32[8,1024]{1,0:T(8,128)}, bf16[1024,384]{1,0:T(8,128)(2,1)}) custom-call(s32[5]{0:T(128)} %stack.57.refs_0_, bf16[2,64,1024]{2,1,0:T(8,128)(2,1)} %copy-done.1, bf16[2,64,1024]{2,1,0:T(8,128)(2,1)} %copy-done.10, ...), custom_call_target="tpu_custom_call" | custom-call | tf_op jit(solution)/shard_map/qkv/pallas_call | solution.py:603
  75.5 5.4 %attention_forward.1 = (bf16[16,64,128]{2,1,0:T(8,128)(2,1)}, f32[1024,128]{1,0:T(8,128)}, f32[1024,128]{1,0:T(8,128)}, bf16[1024,128]{1,0:T(8,128)(2,1)}, bf16[...) custom-call(s32[5]{0:T(128)} %stack.57.refs_0_, bf16[1024,128]{1,0:T(8,128)(2,1)} %get-tuple-element.265.refs_1_, ...), custom_call_target="tpu_custom_call" | custom-call | tf_op jit(solution)/shard_map/attention_forward/pallas_call | solution.py:603
  92.1 4.7 %all-to-all-start.2 = ((bf16[16,64,128]{2,1,0:T(8,128)(2,1)}), bf16[16,64,128]{2,1,0:T(8,128)(2,1)S(1)}, u32[]{:S(2)}, u32[]{:S(2)}) async-start(bf16[16,64,128]{2,1,0:T(8,128)(2,1)} %get-tuple-element.276), calls=%async_computation.2 | async-start | bytes 524288 | tf_op jit(solution)/shard_map/all_to_all | solution.py:1206
  100.6 7.3 %collective-permute-done.21.refs_7_.refs_9_ = bf16[4,32,1024]{2,1,0:T(8,128)(2,1)S(1)} collective-permute-done((bf16[4,32,1024]{2,1,0:T(8,128)(2,1)S(1)}, bf16[4,32,1024]{2,1,0:T(8,128)(2,1)S(1)}, u32[]{:S(2)}, u32[]{:S(2)}) %collective-permute-start.21) | collective-permute-done | bytes 262176 | tf_op jit(solution)/shard_map/ppermute | solution.py:51
  111.7 4.6 %middle.1 = (bf16[128,1024]{1,0:T(8,128)(2,1)}, f32[128,1024]{1,0:T(8,128)}, f32[128,1024]{1,0:T(8,128)}, f32[128,128]{1,0:T(8,128)}, bf16[128,1024]{1,0:T(8,128)(2,1)}) custom-call(s32[5]{0:T(128)} %stack.57.refs_0_, bf16[16,64,128]{2,1,0:T(8,128)(2,1)} %copy-done.23, bf16[2,64,1024]{2,1,0:T(8,128)(2,1)} %refs_3_.1, ...), custom_call_target="tpu_custom_call" | custom-call | tf_op jit(solution)/shard_map/middle/pallas_call | solution.py:603
  123.2 4.9 %collective-permute-done.28.refs_2_ = bf16[128,1024]{1,0:T(8,128)(2,1)S(1)} collective-permute-done((bf16[128,1024]{1,0:T(8,128)(2,1)}, bf16[128,1024]{1,0:T(8,128)(2,1)S(1)}, u32[]{:S(2)}, u32[]{:S(2)}) %collective-permute-start.28) | collective-permute-done | bytes 262176 | tf_op jit(solution)/shard_map/ppermute | solution.py:51
  139.3 9.3 %inner.1 = (bf16[1024,1024]{1,0:T(8,128)(2,1)}, bf16[1024,1024]{1,0:T(8,128)(2,1)}, bf16[512,1024]{1,0:T(8,128)(2,1)}, bf16[1024,512]{1,0:T(8,128)(2,1)}, bf16[1...) custom-call(s32[5]{0:T(128)} %stack.57.refs_0_, ...), custom_call_target="tpu_custom_call" | custom-call | tf_op jit(solution)/shard_map/inner/pallas_call | solution.py:603
  148.9 5.7 %inner_grad.1 = (f32[256,512]{1,0:T(8,128)}, bf16[256,512]{1,0:T(8,128)(2,1)}, bf16[256,512]{1,0:T(8,128)(2,1)}, bf16[256,512]{1,0:T(8,128)(2,1)}) custom-call(s32[5]{0:T(128)} %stack.57.refs_0_, bf16[1024,1024]{1,0:T(8,128)(2,1)} %get-tuple-element.315.refs_1_, bf16[1024,512]{1,0:T(8,128)(2,1)} %get-tuple-element.316.refs_2_), custom_call_target="tpu_custom_call" | custom-call | tf_op jit(solution)/shard_map/inner_grad/pallas_call | solution.py:603
  165.6 7.9 %outer_grad.1 = (f32[128,1024]{1,0:T(8,128)}, bf16[128,1024]{1,0:T(8,128)(2,1)}, bf16[128,1024]{1,0:T(8,128)(2,1)}, bf16[128,1024]{1,0:T(8,128)(2,1)}, f32[512,1024]{1,0:T(8,128)}, /*index=5*/bf16[512,1024]{1,0:T(8,128)(2,1)}) custom-call(s32[5]{0:T(128)} %stack.57.refs_0_, bf16[1024,512]{1,0:T(8,128)(2,1)} %get-tuple-element.325.refs_1_, ...), custom_call_target="tpu_custom_call" | custom-call | tf_op jit(solution)/shard_map/outer_grad/pallas_call | solution.py:603
  178.6 5.3 %branch.1 = (f32[128,1024]{1,0:T(8,128)}, bf16[128,1024]{1,0:T(8,128)(2,1)}, bf16[16,64,128]{2,1,0:T(8,128)(2,1)}, f32[2,1024]{1,0:T(2,128)}) custom-call(s32[5]{0:T(128)} %stack.57.refs_0_, bf16[4,128,1024]{2,1,0:T(8,128)(2,1)} %copy-done, f32[128,1024]{1,0:T(8,128)} %get-tuple-element.336.refs_2_, f32[128,128]{1,0:T(8,128)} %get-tuple-element.337.refs_3_, ...), custom_call_target="tpu_custom_call" | custom-call | tf_op jit(solution)/shard_map/branch/pallas_call | solution.py:603
  188.2 3.9 %all-to-all-start.4 = ((bf16[16,64,128]{2,1,0:T(8,128)(2,1)}), bf16[16,64,128]{2,1,0:T(8,128)(2,1)S(1)}, u32[]{:S(2)}, u32[]{:S(2)}) async-start(bf16[16,64,128]{2,1,0:T(8,128)(2,1)} %get-tuple-element.343), calls=%async_computation.4 | async-start | bytes 524288 | tf_op jit(solution)/shard_map/all_to_all | solution.py:1345
  194.2 5.1 %out_grad.1 = (f32[512,1024]{1,0:T(8,128)}, bf16[512,1024]{1,0:T(8,128)(2,1)}) custom-call(s32[5]{0:T(128)} %stack.57.refs_0_, bf16[128,1024]{1,0:T(8,128)(2,1)} %get-tuple-element.348.refs_1_, bf16[128,1024]{1,0:T(8,128)(2,1)} %get-tuple-element.349.refs_2_), custom_call_target="tpu_custom_call" | custom-call | tf_op jit(solution)/shard_map/out_grad/pallas_call | solution.py:603
  202.3 4.6 %all-to-all-done.4.refs_4_ = bf16[16,64,128]{2,1,0:T(8,128)(2,1)S(1)} async-done(((bf16[16,64,128]{2,1,0:T(8,128)(2,1)}), bf16[16,64,128]{2,1,0:T(8,128)(2,1)S(1)}, u32[]{:S(2)}, u32[]{:S(2)}) %all-to-all-start.4) | async-done | bytes 262176 | tf_op jit(solution)/shard_map/all_to_all | solution.py:1345
  210.6 10.6 %attention_backward.1 = (bf16[1024,128]{1,0:T(8,128)(2,1)}, f32[1024,256]{1,0:T(8,128)}, bf16[1024,256]{1,0:T(8,128)(2,1)}) custom-call(s32[5]{0:T(128)} %stack.57.refs_0_, bf16[1024,128]{1,0:T(8,128)(2,1)} %get-tuple-element.270.refs_1_, bf16[1024,256]{1,0:T(8,128)(2,1)} %get-tuple-element.271.refs_2_, bf16[1024,256]{1,0:T(8,128)(2,1)} %get-tuple-element.272.refs_3_, ...), custom_call_target="tpu_custom_call" | custom-call | tf_op jit(solution)/shard_map/attention_backward/pallas_call | solution.py:603
  228.0 6.3 %partial.1 = (bf16[1024,384]{1,0:T(8,128)(2,1)}, bf16[8,2,64,1024]{3,2,1,0:T(8,128)(2,1)}, f32[2,1024]{1,0:T(2,128)}) custom-call(s32[5]{0:T(128)} %stack.57.refs_0_, bf16[2,64,1024]{2,1,0:T(8,128)(2,1)} %copy-done.1, bf16[2,64,1024]{2,1,0:T(8,128)(2,1)} %copy-done.10, bf16[2,64,1024]{2,1,0:T(8,128)(2,1)} %copy-done.9, bf16[2,64,1024]{2,1,0:T(8,128)(2,1)} %copy-done.14, ...), custom_call_target="tpu_custom_call" | custom-call | tf_op jit(solution)/shard_map/partial/pallas_call | solution.py:603
  239.6 4.6 %all-to-all-start.5 = ((bf16[8,2,64,1024]{3,2,1,0:T(8,128)(2,1)}), bf16[8,2,64,1024]{3,2,1,0:T(8,128)(2,1)}, u32[]{:S(2)}, u32[]{:S(2)}) async-start(bf16[8,2,64,1024]{3,2,1,0:T(8,128)(2,1)} %get-tuple-element.378), calls=%async_computation.5 | async-start | bytes 4194304 | tf_op jit(solution)/shard_map/all_to_all | solution.py:1396
  245.8 5.9 %head_grad.1 = (f32[16,48,384]{2,1,0:T(8,128)}, bf16[16,48,384]{2,1,0:T(8,128)(2,1)}) custom-call(s32[5]{0:T(128)} %stack.57.refs_0_, bf16[1024,1024]{1,0:T(8,128)(2,1)} %get-tuple-element.379.refs_1_, bf16[1024,384]{1,0:T(8,128)(2,1)} %get-tuple-element.380.refs_2_, f32[32,128]{1,0:T(8,128)} %reshape.313.refs_3_), custom_call_target="tpu_custom_call" | custom-call | tf_op jit(solution)/shard_map/head_grad/pallas_call | solution.py:603
  262.5 9.2 %collective-permute-done.58 = bf16[4,32,1024]{2,1,0:T(8,128)(2,1)S(1)} collective-permute-done((bf16[4,32,1024]{2,1,0:T(8,128)(2,1)S(1)}, bf16[4,32,1024]{2,1,0:T(8,128)(2,1)S(1)}, u32[]{:S(2)}, u32[]{:S(2)}) %collective-permute-start.58) | collective-permute-done | bytes 262176 | tf_op jit(solution)/shard_map/ppermute | solution.py:51
  271.7 7.2 %collective-permute-done.60 = bf16[128,1024]{1,0:T(8,128)(2,1)S(1)} collective-permute-done((bf16[128,1024]{1,0:T(8,128)(2,1)S(1)}, bf16[128,1024]{1,0:T(8,128)(2,1)S(1)}, u32[]{:S(2)}, u32[]{:S(2)}) %collective-permute-start.60) | collective-permute-done | bytes 262176 | tf_op jit(solution)/shard_map/ppermute | solution.py:51
  288.4 4.6 %all-to-all-start.6 = ((bf16[8,48,384]{2,1,0:T(8,128)(2,1)}), bf16[8,48,384]{2,1,0:T(8,128)(2,1)S(1)}, u32[]{:S(2)}, u32[]{:S(2)}) async-start(bf16[8,48,384]{2,1,0:T(8,128)(2,1)} %payload.1), calls=%async_computation.6 | async-start | bytes 589824 | tf_op jit(solution)/shard_map/all_to_all | solution.py:1452
  (323 shorter events, 159.8 us)
Async XLA Ops:
  22.1 26.9 %all-to-all-start = ((bf16[16,112,128]{2,1,0:T(8,128)(2,1)}), bf16[16,112,128]{2,1,0:T(8,128)(2,1)S(1)}, u32[]{:S(2)}, u32[]{:S(2)}) async-start(bf16[16,112,128]{2,1,0:T(8,128)(2,1)} %get-tuple-element.248), calls=%async_computation | async-start | bytes 917504 | tf_op jit(solution)/shard_map/all_to_all | solution.py:1159
  27.8 19.2 %collective-permute-start.7 = (bf16[2,64,1024]{2,1,0:T(8,128)(2,1)S(1)}, bf16[2,64,1024]{2,1,0:T(8,128)(2,1)S(1)}, u32[]{:S(2)}, u32[]{:S(2)}) collective-permute-start(bf16[2,64,1024]{2,1,0:T(8,128)(2,1)S(1)} %pad_maximum_fusion.refs_1_), channel_id=1, source_target_pairs={{0,22},{2,20},{4,18},{6,16},{16,6},{18,4},{20,2},{22,0},{1,23},{3,... | collective-permute-start | bytes 786440 | tf_op jit(solution)/shard_map/ppermute | solution.py:1158
  31.5 17.4 %collective-permute-start.4 = (bf16[2,64,1024]{2,1,0:T(8,128)(2,1)S(1)}, bf16[2,64,1024]{2,1,0:T(8,128)(2,1)S(1)}, u32[]{:S(2)}, u32[]{:S(2)}) collective-permute-start(bf16[2,64,1024]{2,1,0:T(8,128)(2,1)S(1)} %collective-permute-done.1.refs_5_), channel_id=1, source_target_pairs={{0,4},{4,0},{1,5},{5,1},{2,6},{6,2},{3,7},{7,3},{8,12},{12,8},{9,1... | collective-permute-start | bytes 786440 | tf_op jit(solution)/shard_map/ppermute | solution.py:51
  32.1 16.8 %collective-permute-start.5 = (bf16[2,64,1024]{2,1,0:T(8,128)(2,1)S(1)}, bf16[2,64,1024]{2,1,0:T(8,128)(2,1)S(1)}, u32[]{:S(2)}, u32[]{:S(2)}) collective-permute-start(bf16[2,64,1024]{2,1,0:T(8,128)(2,1)S(1)} %collective-permute-done.3.refs_2_), channel_id=1, source_target_pairs={{0,16},{16,0},{1,17},{17,1},{2,18},{18,2},{3,19},{19,3},{4,20},{20... | collective-permute-start | bytes 786440 | tf_op jit(solution)/shard_map/ppermute | solution.py:51
  32.7 16.3 %collective-permute-start.6 = (bf16[2,64,1024]{2,1,0:T(8,128)(2,1)S(1)}, bf16[2,64,1024]{2,1,0:T(8,128)(2,1)S(1)}, u32[]{:S(2)}, u32[]{:S(2)}) collective-permute-start(bf16[2,64,1024]{2,1,0:T(8,128)(2,1)S(1)} %collective-permute-done.2.refs_3_), channel_id=1, source_target_pairs={{0,2},{2,0},{1,3},{3,1},{4,6},{6,4},{5,7},{7,5},{8,10},{10,8},{9,1... | collective-permute-start | bytes 786440 | tf_op jit(solution)/shard_map/ppermute | solution.py:51
  50.8 16.6 %collective-permute-start.11 = (bf16[128,1024]{1,0:T(8,128)(2,1)}, bf16[128,1024]{1,0:T(8,128)(2,1)}, u32[]{:S(2)}, u32[]{:S(2)}) collective-permute-start(bf16[128,1024]{1,0:T(8,128)(2,1)} %refs_25_), channel_id=1, source_target_pairs={{0,8},{8,0},{1,9},{9,1},{2,10},{10,2},{3,11},{11,3},{4,12},{12,4},... | collective-permute-start | bytes 786440 | tf_op jit(solution)/shard_map/ppermute | solution.py:51
  52.5 15.0 %collective-permute-start.12 = (bf16[128,1024]{1,0:T(8,128)(2,1)}, bf16[128,1024]{1,0:T(8,128)(2,1)}, u32[]{:S(2)}, u32[]{:S(2)}) collective-permute-start(bf16[128,1024]{1,0:T(8,128)(2,1)} %refs_25_), channel_id=1, source_target_pairs={{0,4},{4,0},{1,5},{5,1},{2,6},{6,2},{3,7},{7,3},{8,12},{12,8},{9,1... | collective-permute-start | bytes 786440 | tf_op jit(solution)/shard_map/ppermute | solution.py:51
  71.9 14.3 %collective-permute-start.16 = (bf16[8,32,512]{2,1,0:T(8,128)(2,1)S(1)}, bf16[8,32,512]{2,1,0:T(8,128)(2,1)S(1)}, u32[]{:S(2)}, u32[]{:S(2)}) collective-permute-start(bf16[8,32,512]{2,1,0:T(8,128)(2,1)S(1)} %all-to-all-done.1), channel_id=1, source_target_pairs={{0,8},{8,0},{1,9},{9,1},{2,10},{10,2},{3,11},{11,3},{4,12},{12,4},... | collective-permute-start | bytes 786440 | tf_op jit(solution)/shard_map/ppermute | solution.py:51
  73.5 16.6 %collective-permute-start.17 = (bf16[8,32,512]{2,1,0:T(8,128)(2,1)S(1)}, bf16[8,32,512]{2,1,0:T(8,128)(2,1)S(1)}, u32[]{:S(2)}, u32[]{:S(2)}) collective-permute-start(bf16[8,32,512]{2,1,0:T(8,128)(2,1)S(1)} %all-to-all-done.1), channel_id=1, source_target_pairs={{0,4},{4,0},{1,5},{5,1},{2,6},{6,2},{3,7},{7,3},{8,12},{12,8},{9,1... | collective-permute-start | bytes 786440 | tf_op jit(solution)/shard_map/ppermute | solution.py:51
  75.5 21.4 %collective-permute-start.22 = (bf16[128,1024]{1,0:T(8,128)(2,1)}, bf16[128,1024]{1,0:T(8,128)(2,1)}, u32[]{:S(2)}, u32[]{:S(2)}) collective-permute-start(bf16[128,1024]{1,0:T(8,128)(2,1)} %collective-permute-done.11.refs_27_), channel_id=1, source_target_pairs={{0,4},{4,0},{1,5},{5,1},{2,6},{6,2},{3,7},{7,3},{8,12},{12,8},{9,1... | collective-permute-start | bytes 786440 | tf_op jit(solution)/shard_map/ppermute | solution.py:51
  83.8 15.1 %collective-permute-start.24 = (bf16[4,32,1024]{2,1,0:T(8,128)(2,1)S(1)}, bf16[4,32,1024]{2,1,0:T(8,128)(2,1)S(1)}, u32[]{:S(2)}, u32[]{:S(2)}) collective-permute-start(bf16[4,32,1024]{2,1,0:T(8,128)(2,1)S(1)} %pad_maximum_fusion.1.refs_4_.refs_6_), channel_id=1, source_target_pairs={{0,1},{1,0},{2,3},{3,2},{4,5},{5,4},{6,7},{7,6},{8,9},{9,8},{10,11... | collective-permute-start | bytes 786440 | tf_op jit(solution)/shard_map/ppermute | solution.py:51
  92.1 17.2 %all-to-all-start.2 = ((bf16[16,64,128]{2,1,0:T(8,128)(2,1)}), bf16[16,64,128]{2,1,0:T(8,128)(2,1)S(1)}, u32[]{:S(2)}, u32[]{:S(2)}) async-start(bf16[16,64,128]{2,1,0:T(8,128)(2,1)} %get-tuple-element.276), calls=%async_computation.2 | async-start | bytes 524288 | tf_op jit(solution)/shard_map/all_to_all | solution.py:1206
  159.3 18.3 %all-to-all-start.3 = ((bf16[4,128,1024]{2,1,0:T(8,128)(2,1)}), bf16[4,128,1024]{2,1,0:T(8,128)(2,1)S(1)}, u32[]{:S(2)}, u32[]{:S(2)}) async-start(bf16[4,128,1024]{2,1,0:T(8,128)(2,1)} %fold.1), calls=%async_computation.3 | async-start | bytes 2097152 | tf_op jit(solution)/shard_map/all_to_all | solution.py:1305
  163.2 14.4 %collective-permute-start.45 = (bf16[256,512]{1,0:T(8,128)(2,1)S(1)}, bf16[256,512]{1,0:T(8,128)(2,1)}, u32[]{:S(2)}, u32[]{:S(2)}) collective-permute-start(bf16[256,512]{1,0:T(8,128)(2,1)S(1)} %copy-done.72), channel_id=1, source_target_pairs={{0,8},{8,0},{1,9},{9,1},{2,10},{10,2},{3,11},{11,3},{4,12},{12,4},... | collective-permute-start | bytes 786440 | tf_op jit(solution)/shard_map/ppermute | solution.py:51
  184.0 16.1 %collective-permute-start.47 = (bf16[128,1024]{1,0:T(8,128)(2,1)}, bf16[128,1024]{1,0:T(8,128)(2,1)}, u32[]{:S(2)}, u32[]{:S(2)}) collective-permute-start(bf16[128,1024]{1,0:T(8,128)(2,1)} %get-tuple-element.344), channel_id=1, source_target_pairs={{0,4},{4,0},{1,5},{5,1},{2,6},{6,2},{3,7},{7,3},{8,12},{12,8},{9,1... | collective-permute-start | bytes 786440 | tf_op jit(solution)/shard_map/ppermute | solution.py:51
  185.6 16.7 %collective-permute-start.48 = (bf16[128,1024]{1,0:T(8,128)(2,1)}, bf16[128,1024]{1,0:T(8,128)(2,1)}, u32[]{:S(2)}, u32[]{:S(2)}) collective-permute-start(bf16[128,1024]{1,0:T(8,128)(2,1)} %get-tuple-element.345), channel_id=1, source_target_pairs={{0,8},{8,0},{1,9},{9,1},{2,10},{10,2},{3,11},{11,3},{4,12},{12,4},... | collective-permute-start | bytes 786440 | tf_op jit(solution)/shard_map/ppermute | solution.py:51
  188.2 18.6 %all-to-all-start.4 = ((bf16[16,64,128]{2,1,0:T(8,128)(2,1)}), bf16[16,64,128]{2,1,0:T(8,128)(2,1)S(1)}, u32[]{:S(2)}, u32[]{:S(2)}) async-start(bf16[16,64,128]{2,1,0:T(8,128)(2,1)} %get-tuple-element.343), calls=%async_computation.4 | async-start | bytes 524288 | tf_op jit(solution)/shard_map/all_to_all | solution.py:1345
  206.9 14.4 %collective-permute-start.51 = (bf16[512,1024]{1,0:T(8,128)(2,1)}, bf16[512,1024]{1,0:T(8,128)(2,1)S(1)}, u32[]{:S(2)}, u32[]{:S(2)}) collective-permute-start(bf16[512,1024]{1,0:T(8,128)(2,1)} %get-tuple-element.362), channel_id=1, source_target_pairs={{0,1},{1,0},{2,3},{3,2},{4,5},{5,4},{6,7},{7,6},{8,9},{9,8},{10,11... | collective-permute-start | bytes 3145736 | tf_op jit(solution)/shard_map/ppermute | solution.py:51
  206.9 14.4 %collective-permute-start.52 = (bf16[256,512]{1,0:T(8,128)(2,1)}, bf16[256,512]{1,0:T(8,128)(2,1)S(1)}, u32[]{:S(2)}, u32[]{:S(2)}) collective-permute-start(bf16[256,512]{1,0:T(8,128)(2,1)} %get-tuple-element.363), channel_id=1, source_target_pairs={{0,12},{4,8},{8,4},{12,0},{1,13},{5,9},{9,5},{13,1},{2,14},{6,10},... | collective-permute-start | bytes 786440 | tf_op jit(solution)/shard_map/ppermute | solution.py:1371
  239.6 43.4 %all-to-all-start.5 = ((bf16[8,2,64,1024]{3,2,1,0:T(8,128)(2,1)}), bf16[8,2,64,1024]{3,2,1,0:T(8,128)(2,1)}, u32[]{:S(2)}, u32[]{:S(2)}) async-start(bf16[8,2,64,1024]{3,2,1,0:T(8,128)(2,1)} %get-tuple-element.378), calls=%async_computation.5 | async-start | bytes 4194304 | tf_op jit(solution)/shard_map/all_to_all | solution.py:1396
  255.1 23.8 %collective-permute-start.57 = (bf16[2,192,384]{2,1,0:T(8,128)(2,1)S(1)}, bf16[2,192,384]{2,1,0:T(8,128)(2,1)S(1)}, u32[]{:S(2)}, u32[]{:S(2)}) collective-permute-start(bf16[2,192,384]{2,1,0:T(8,128)(2,1)S(1)} %get-tuple-element.401), channel_id=1, source_target_pairs={{0,8},{8,0},{1,9},{9,1},{2,10},{10,2},{3,11},{11,3},{4,12},{12,4},... | collective-permute-start | bytes 884744 | tf_op jit(solution)/shard_map/ppermute | solution.py:51
  257.4 14.3 %collective-permute-start.58 = (bf16[4,32,1024]{2,1,0:T(8,128)(2,1)S(1)}, bf16[4,32,1024]{2,1,0:T(8,128)(2,1)S(1)}, u32[]{:S(2)}, u32[]{:S(2)}) collective-permute-start(bf16[4,32,1024]{2,1,0:T(8,128)(2,1)S(1)} %get-tuple-element.403), channel_id=1, source_target_pairs={{0,2},{2,0},{1,3},{3,1},{4,6},{6,4},{5,7},{7,5},{8,10},{10,8},{9,1... | collective-permute-start | bytes 786440 | tf_op jit(solution)/shard_map/ppermute | solution.py:51
  259.0 19.9 %collective-permute-start.60 = (bf16[128,1024]{1,0:T(8,128)(2,1)S(1)}, bf16[128,1024]{1,0:T(8,128)(2,1)S(1)}, u32[]{:S(2)}, u32[]{:S(2)}) collective-permute-start(bf16[128,1024]{1,0:T(8,128)(2,1)S(1)} %pad_maximum_fusion.2), channel_id=1, source_target_pairs={{0,16},{16,0},{1,17},{17,1},{2,18},{18,2},{3,19},{19,3},{4,20},{20... | collective-permute-start | bytes 786440 | tf_op jit(solution)/shard_map/ppermute | solution.py:51
  288.4 17.0 %all-to-all-start.6 = ((bf16[8,48,384]{2,1,0:T(8,128)(2,1)}), bf16[8,48,384]{2,1,0:T(8,128)(2,1)S(1)}, u32[]{:S(2)}, u32[]{:S(2)}) async-start(bf16[8,48,384]{2,1,0:T(8,128)(2,1)} %payload.1), calls=%async_computation.6 | async-start | bytes 589824 | tf_op jit(solution)/shard_map/all_to_all | solution.py:1452
  (124 other events, 1156.6 us)
